TPU v7x, 256 devices: a whole 4x4x8 slice. The times are simulated.
256 devices in a mesh: gx: 16 (over y_lo, z), gy: 16 (over x, y_hi, core).
Axes of the slice: x: 4, y: 4 (y_hi: 2, y_lo: 2; y = y_hi * 2 + y_lo), z: 8, core: 2. Of those that a mesh axis runs over, the one named last changes fastest.
Arguments:
- tokens: bfloat16 [4, 128, 128, 256], P(None, 'gx', 'gy'), may hold values from -6 to 6
- syndrome: int32 [4, 128, 128], P(None, 'gx', 'gy'), may hold values 0 or 1
- check_plan_step: int32 [4, 128, 128], P(None, 'gx', 'gy'), may hold values from 0 to 7
- offsets: int32 [6, 2], replicated, may hold values from 0 to 8, as said below
- flip_vector: float32 [256], replicated, may hold values from -3 to 3
- plan_step_embedding: float32 [8, 256], replicated, may hold values from -3 to 3
- gain_tanner: float32 [256], replicated, may hold values from 0.5 to 1.5
- w_query: bfloat16 [256, 256], replicated, may hold values from -0.375 to 0.375
- w_key_value: bfloat16 [256, 512], replicated, may hold values from -0.375 to 0.375
- w_merge: bfloat16 [256, 256], replicated, may hold values from -0.375 to 0.375
- gain_time: float32 [256], replicated, may hold values from 0.5 to 1.5
- w_temporal: bfloat16 [256, 768], replicated, may hold values from -0.375 to 0.375
- w_temporal_out: bfloat16 [256, 256], replicated, may hold values from -0.375 to 0.375
- gain_ffn: float32 [256], replicated, may hold values from 0.5 to 1.5
- w_ffn_up: bfloat16 [256, 1024], replicated, may hold values from -0.375 to 0.375
- w_ffn_down: bfloat16 [1024, 256], replicated, may hold values from -0.1875 to 0.1875
- cotangent: bfloat16 [4, 128, 128, 256], P(None, 'gx', 'gy'), may hold values from -6 to 6
Outputs:
- token_grad: bfloat16 [4, 128, 128, 256], P(None, 'gx', 'gy')
- grad_flip: float32 [256], replicated
- plan_step_gradient: float32 [8, 256], replicated
- grad_gain_tanner: float32 [256], replicated
- grad_query: float32 [256, 256], replicated
- grad_key_value: float32 [256, 512], replicated
- grad_merge: float32 [256, 256], replicated
- grad_gain_time: float32 [256], replicated
- grad_temporal: float32 [256, 768], replicated
- grad_temporal_out: float32 [256, 256], replicated
- grad_gain_ffn: float32 [256], replicated
- grad_up: float32 [256, 1024], replicated
- grad_down: float32 [1024, 256], replicated
Inputs may be any that keep to these rules, and one draw needn't show every extreme that they name: `offsets`: rows 0, 4 and 5 are (e, 0) and rows 1, 2 and 3 are (0, e), with e from 1 to 8; rows 0 and 3 have e = 8.
All inputs are finite; a program needn't handle non-finite values. No bound on the sum of `syndrome` on one device may be relied on, other than what follows from the above.
Results may differ from a plain program's by a relative error of at most 0.022.
Values may be sent and summed in bfloat16 or wider, within the bound.
A program may use at most 64 MiB of HBM per device.

v0:
```python
import math

import jax
import jax.numpy as jnp
from jax import lax
from jax.sharding import PartitionSpec as P

MODEL_WIDTH = 256
HEADDIM = 32
PLAN_STEP_COUNT = 8
MONOS = 6
MAXEXP = 8


EPS = 1e-05
CAP = 4.0
EXACT_PRECISION = lax.Precision.HIGHEST
ALONG_ROWS = (0, 4, 5)


def shifted(x, axis, by):
    count = lax.axis_size(axis)
    return lax.ppermute(x, axis, [(i, (i + by) % count) for i in range(count)])


def rms_norm(stream, gain):
    return stream * lax.rsqrt(jnp.mean(stream * stream, axis=-1, keepdims=True) + EPS) * gain


def matmul(inputs, weight):
    return lax.dot_general(
        inputs, weight, (((inputs.ndim - 1,), (0,)), ((), ())), preferred_element_type=jnp.float32
    )


def back_matmul(inputs, weight, grad_result):
    grad_low = grad_result.astype(jnp.bfloat16)
    grad_inputs = lax.dot_general(
        grad_low,
        weight,
        (((grad_low.ndim - 1,), (1,)), ((), ())),
        preferred_element_type=jnp.float32,
    )
    flat_inputs = inputs.reshape(-1, inputs.shape[-1])
    flat_grad = grad_low.reshape(-1, grad_low.shape[-1])
    grad_weight = lax.dot_general(
        flat_inputs, flat_grad, (((0,), (0,)), ((), ())), preferred_element_type=jnp.float32
    )
    return (grad_inputs, grad_weight)


def head_total(product):
    width = product.shape[-1]
    row_head = lax.broadcasted_iota(jnp.int32, (width, width), 0) // HEADDIM
    col_head = lax.broadcasted_iota(jnp.int32, (width, width), 1) // HEADDIM
    block = (row_head == col_head).astype(jnp.float32)
    return lax.dot_general(
        product, block, (((product.ndim - 1,), (0,)), ((), ())), precision=EXACT_PRECISION
    )


def attend(query, moved):
    weights = []
    for neighbour in moved:
        score = head_total(query * neighbour[..., :MODEL_WIDTH]) / math.sqrt(HEADDIM)
        weights.append(jnp.exp(CAP * jnp.tanh(score / CAP)))
    normalizer = weights[0]
    for weight in weights[1:]:
        normalizer = normalizer + weight
    mixed = jnp.zeros(query.shape, jnp.float32)
    for weight, neighbour in zip(weights, moved):
        mixed = mixed + weight / normalizer * neighbour[..., MODEL_WIDTH:]
    return mixed


def tanner_local(query, key_value, next_rows, next_cols, offsets):
    extended_rows = jnp.concatenate([key_value, next_rows], axis=1)
    extended_cols = jnp.concatenate([key_value, next_cols], axis=2)
    moved = [key_value]
    for index in range(MONOS):
        if index in ALONG_ROWS:
            moved.append(
                lax.dynamic_slice_in_dim(extended_rows, offsets[index, 0], key_value.shape[1], 1)
            )
        else:
            moved.append(
                lax.dynamic_slice_in_dim(extended_cols, offsets[index, 1], key_value.shape[2], 2)
            )
    return attend(query, moved)


def time_attend(packed):
    queries = packed[..., :MODEL_WIDTH]
    keys = packed[..., MODEL_WIDTH : 2 * MODEL_WIDTH]
    values = packed[..., 2 * MODEL_WIDTH :]
    outputs = []
    for later in range(packed.shape[0]):
        weights = []
        for earlier in range(later + 1):
            score = head_total(queries[later] * keys[earlier]) / math.sqrt(HEADDIM)
            weights.append(jnp.exp(CAP * jnp.tanh(score / CAP)))
        normalizer = weights[0]
        for weight in weights[1:]:
            normalizer = normalizer + weight
        mixed = jnp.zeros(queries.shape[1:], jnp.float32)
        for earlier in range(later + 1):
            mixed = mixed + weights[earlier] / normalizer * values[earlier]
        outputs.append(mixed)
    return jnp.stack(outputs, axis=0)


def on_device(
    tokens,
    syndrome,
    check_plan_step,
    offsets,
    flip_vector,
    plan_step_embedding,
    gain_tanner,
    w_query,
    w_key_value,
    w_merge,
    gain_time,
    w_temporal,
    w_temporal_out,
    gain_ffn,
    w_ffn_up,
    w_ffn_down,
    cotangent,
):
    plan_step_onehot = (
        check_plan_step[..., None] == jnp.arange(PLAN_STEP_COUNT, dtype=jnp.int32)
    ).astype(jnp.float32)
    syndrome_float = syndrome.astype(jnp.float32)
    embedded = (
        tokens.astype(jnp.float32)
        + syndrome_float[..., None] * flip_vector
        + jnp.dot(plan_step_onehot, plan_step_embedding, precision=EXACT_PRECISION)
    )
    normed_one, norm_one_back = jax.vjp(rms_norm, embedded, gain_tanner)
    hidden_one = normed_one.astype(jnp.bfloat16)
    query = matmul(hidden_one, w_query).astype(jnp.bfloat16)
    key_value = matmul(hidden_one, w_key_value).astype(jnp.bfloat16)
    next_rows = shifted(key_value, "gx", -1)
    next_cols = shifted(key_value, "gy", -1)

    def tanner_part(query_in, key_in, rows_in, cols_in):
        return tanner_local(query_in, key_in, rows_in, cols_in, offsets)

    mixed_float, tanner_back = jax.vjp(
        tanner_part,
        query.astype(jnp.float32),
        key_value.astype(jnp.float32),
        next_rows.astype(jnp.float32),
        next_cols.astype(jnp.float32),
    )
    mixed_one = mixed_float.astype(jnp.bfloat16)
    after_tanner = embedded + matmul(mixed_one, w_merge)
    normed_two, norm_two_back = jax.vjp(rms_norm, after_tanner, gain_time)
    hidden_two = normed_two.astype(jnp.bfloat16)
    packed = matmul(hidden_two, w_temporal).astype(jnp.bfloat16)
    mixed_time, time_back = jax.vjp(time_attend, packed.astype(jnp.float32))
    mixed_two = mixed_time.astype(jnp.bfloat16)
    after_time = after_tanner + matmul(mixed_two, w_temporal_out)
    normed_three, norm_three_back = jax.vjp(rms_norm, after_time, gain_ffn)
    hidden_three = normed_three.astype(jnp.bfloat16)
    before_act = matmul(hidden_three, w_ffn_up)
    activated_float, gelu_back = jax.vjp(jax.nn.gelu, before_act)
    activated = activated_float.astype(jnp.bfloat16)
    grad_output = cotangent.astype(jnp.float32)
    grad_act, grad_down = back_matmul(activated, w_ffn_down, grad_output)
    grad_before = gelu_back(grad_act)[0]
    grad_three, grad_up = back_matmul(hidden_three, w_ffn_up, grad_before)
    grad_norm_three, grad_gain_ffn = norm_three_back(grad_three)
    grad_after_time = grad_output + grad_norm_three
    grad_mixed_two, grad_temporal_out = back_matmul(mixed_two, w_temporal_out, grad_after_time)
    grad_packed = time_back(grad_mixed_two)[0]
    grad_two, grad_temporal = back_matmul(hidden_two, w_temporal, grad_packed)
    grad_norm_two, grad_gain_time = norm_two_back(grad_two)
    grad_after_tanner = grad_after_time + grad_norm_two
    scale = 1.0 / math.sqrt(
        tokens.shape[0]
        * tokens.shape[1]
        * tokens.shape[2]
        * lax.axis_size("gx")
        * lax.axis_size("gy")
    )
    grad_mixed_one, grad_merge = back_matmul(mixed_one, w_merge, grad_after_tanner)
    grad_query_out, grad_key_local, grad_rows, grad_cols = tanner_back(grad_mixed_one)
    back_rows = shifted(grad_rows.astype(jnp.bfloat16), "gx", 1).astype(grad_rows.dtype)
    back_cols = shifted(grad_cols.astype(jnp.bfloat16), "gy", 1).astype(grad_cols.dtype)
    grad_key_out = grad_key_local.at[:, :MAXEXP].add(back_rows)
    grad_key_out = grad_key_out.at[:, :, :MAXEXP].add(back_cols)
    grad_one_key, grad_key_value = back_matmul(hidden_one, w_key_value, grad_key_out)
    grad_one_query, grad_query = back_matmul(hidden_one, w_query, grad_query_out)
    grad_norm_one, grad_gain_tanner = norm_one_back(grad_one_query + grad_one_key)
    embedding_gradient = grad_after_tanner + grad_norm_one
    token_grad = embedding_gradient.astype(jnp.bfloat16)
    grad_flip = jnp.sum(syndrome_float[..., None] * embedding_gradient, axis=(0, 1, 2))
    plan_step_gradient = lax.dot_general(
        plan_step_onehot.reshape(-1, PLAN_STEP_COUNT),
        embedding_gradient.reshape(-1, MODEL_WIDTH),
        (((0,), (0,)), ((), ())),
        precision=EXACT_PRECISION,
    )
    summed = lax.psum(
        (
            grad_flip * scale,
            plan_step_gradient * scale,
            grad_gain_tanner * scale,
            grad_query * scale,
            grad_key_value * scale,
            grad_merge * scale,
            grad_gain_time * scale,
            grad_temporal * scale,
            grad_temporal_out * scale,
            grad_gain_ffn * scale,
            grad_up * scale,
            grad_down * scale,
        ),
        ("gx", "gy"),
    )
    return (
        token_grad,
        summed[0],
        summed[1],
        summed[2],
        summed[3],
        summed[4],
        summed[5],
        summed[6],
        summed[7],
        summed[8],
        summed[9],
        summed[10],
        summed[11],
    )


def solution(mesh):
    return jax.shard_map(
        on_device,
        mesh=mesh,
        in_specs=(
            P(None, "gx", "gy", None),
            P(None, "gx", "gy"),
            P(None, "gx", "gy"),
            P(),
            P(),
            P(),
            P(),
            P(),
            P(),
            P(),
            P(),
            P(),
            P(),
            P(),
            P(),
            P(),
            P(None, "gx", "gy", None),
        ),
        out_specs=(
            P(None, "gx", "gy", None),
            P(),
            P(),
            P(),
            P(),
            P(),
            P(),
            P(),
            P(),
            P(),
            P(),
            P(),
            P(),
        ),
        check_vma=False,
    )
```

profile of v0, /device:TPU:1, one launch (start us, length us, event | category | flops | bytes accessed | tf_op | source)
XLA Modules:
  0.0 367.5 jit_solution(12279995785802206643)
XLA Ops:
  7.3 0.8 convert_element_type.99
  8.0 0.6 copy-done.21
  8.7 1.3 multiply_reduce_fusion.9
  11.2 7.5 %collective-permute-start = (bf16[4,8,8,512]{3,2,1,0:T(8,128)(2,1)S(1)}, bf16[4,8,8,512]{3,2,1,0:T(8,128)(2,1)S(1)}, u32[]{:S(2)}, u32[]{:S(2)}) collective-permute-start(bf16[4,8,8,512]{3,2,1,0:T(8,128)(2,1)S(1)} %get-tuple-element.163), channel_id=1, source_target_pairs={{0,240},{16,0},{32,16},{48,32},{64,48},{80,64},{96,80},{112,96},{1... | collective-permute-start | bytes 786440 | tf_op jit(solution)/shard_map/ppermute | solution.py:23
  18.7 1.0 collective-permute-start.1
  19.6 0.6 fusion.486
  32.2 0.8 fusion.38
  35.7 0.8 add_convert_fusion.2
  42.0 0.8 copy-done.7
  43.1 0.7 copy-done.31
  44.9 0.9 fusion.33
  45.7 0.9 multiply_reduce_fusion
  46.8 0.9 fusion.12
  52.4 1.3 fusion.2
  53.7 1.1 multiply_reduce_fusion.1
  54.9 1.9 fusion.472
  59.9 1.4 fusion.1
  61.3 1.5 fusion
  62.8 1.6 fusion.485
  64.6 0.9 dynamic_update_slice.22
  65.5 1.2 add_add_fusion.1
  66.7 1.0 add_any.332
  67.7 1.2 add_add_fusion
  68.9 1.0 add_any.335
  70.0 2.6 collective-permute-start.3
  72.7 0.8 copy-done.3
  73.6 0.9 copy-done.17
  74.6 0.9 copy-done.16
  75.7 0.8 copy-done.9
  76.5 0.9 fusion.14
  77.4 0.9 fusion.13
  78.4 5.5 %collective-permute-done.2 = bf16[4,8,8,512]{3,2,1,0:T(8,128)(2,1)S(1)} collective-permute-done((bf16[4,8,8,512]{3,2,1,0:T(8,128)(2,1)S(1)}, bf16[4,8,8,512]{3,2,1,0:T(8,128)(2,1)S(1)}, u32[]{:S(2)}, u32[]{:S(2)}) %collective-permute-start.2) | collective-permute-done | bytes 262176 | tf_op jit(solution)/shard_map/ppermute | solution.py:23
  84.1 1.1 fusion.4
  85.2 0.7 copy-done.39
  85.9 0.7 copy-done.37
  86.8 0.7 copy-done.5
  88.2 0.7 copy-done.22
  89.1 0.7 convert_element_type.120
  90.2 76.5 %all-reduce.47 = (f32[256]{0:T(256)}, f32[8,256]{1,0:T(8,128)}, f32[256]{0:T(256)}, f32[256]{0:T(256)}, f32[256]{0:T(256)}) all-reduce(f32[256]{0:T(256)S(1)} %broadcast_multiply_fusion.3, f32[8,256]{1,0:T(8,128)S(1)} %fusion.26, f32[256]{0:T(256)S(1)} %broadcast_multiply_fusion.2, ...), channel_id=1, replica_groups=mesh['gx'=16,'gy'=16] {'gx','gy'}, use_global_device_ids=true, to_apply=%region_7.8 | all-reduce | flops 3072 | bytes 24576 | tf_op jit(solution)/shard_map/psum | solution.py:206
  166.7 186.1 %all-reduce.51.cloned.1.call-done = (f32[256,256]{1,0:T(8,128)}, f32[256,512]{1,0:T(8,128)}, f32[256,256]{1,0:T(8,128)}, f32[256,768]{1,0:T(8,128)}, f32[256,256...) async-done(((f32[256,256]{1,0:T(8,128)}, f32[256,512]{1,0:T(8,128)}, f32[256,256]{1,0:T(8,128)}, f32[256,768]{1,0:T(8,128)}, f32[256,256]{1,0:T(8,128)}, ...) | async-done | bytes 4194320 | tf_op jit(solution)/shard_map/psum | solution.py:206
  352.8 1.7 copy.62
  354.5 0.8 copy.63
  355.6 0.7 copy.64
  356.3 0.9 copy.65
  357.4 0.7 copy.66
  358.1 1.0 copy.67
  359.1 0.6 copy-done.1
  359.7 1.0 copy.68
  (152 shorter events, 21.7 us)
Async XLA Ops:
  7.2 35.9 %copy-start = (bf16[256,1024]{1,0:T(8,128)(2,1)S(1)}, bf16[256,1024]{1,0:T(8,128)(2,1)}, u32[]{:S(2)}) copy-start(bf16[256,1024]{1,0:T(8,128)(2,1)} %param.39) | copy-start | bytes 1572868
  7.2 1.4 copy-start.29
  7.2 1.4 copy-start.38
  7.2 1.4 copy-start.35
  7.2 345.6 %all-reduce.51.cloned.1.call-start = ((), (), s32[]{:S(2)}) async-start(), calls=%async_computation | async-start | bytes 8388608 | tf_op jit(solution)/shard_map/psum | solution.py:206
  8.0 0.6 copy-start.21
  8.6 1.9 copy-start.33
  10.0 0.6 copy-start.23
  10.0 1.0 copy-start.4
  10.9 21.0 %copy-start.10 = (bf16[256,256]{1,0:T(8,128)(2,1)S(1)}, bf16[256,256]{1,0:T(8,128)(2,1)}, u32[]{:S(2)}) copy-start(bf16[256,256]{1,0:T(8,128)(2,1)} %param.32) | copy-start | bytes 393220
  11.2 8.5 %copy-start.32 = (s32[6,2]{0,1:T(2,128)S(1)}, s32[6,2]{0,1:T(2,128)}, u32[]{:S(2)}) copy-start(s32[6,2]{0,1:T(2,128)} %param.28) | copy-start | bytes 148
  11.2 20.9 %collective-permute-start = (bf16[4,8,8,512]{3,2,1,0:T(8,128)(2,1)S(1)}, bf16[4,8,8,512]{3,2,1,0:T(8,128)(2,1)S(1)}, u32[]{:S(2)}, u32[]{:S(2)}) collective-permute-start(bf16[4,8,8,512]{3,2,1,0:T(8,128)(2,1)S(1)} %get-tuple-element.163), channel_id=1, source_target_pairs={{0,240},{16,0},{32,16},{48,32},{64,48},{80,64},{96,80},{112,96},{1... | collective-permute-start | bytes 786440 | tf_op jit(solution)/shard_map/ppermute | solution.py:23
  18.7 13.5 %collective-permute-start.1 = (bf16[4,8,8,512]{3,2,1,0:T(8,128)(2,1)S(1)}, bf16[4,8,8,512]{3,2,1,0:T(8,128)(2,1)S(1)}, u32[]{:S(2)}, u32[]{:S(2)}) collective-permute-start(bf16[4,8,8,512]{3,2,1,0:T(8,128)(2,1)S(1)} %get-tuple-element.163), channel_id=1, source_target_pairs={{0,15},{1,0},{2,1},{3,2},{4,3},{5,4},{6,5},{7,6},{8,7},{9,8},{10,9... | collective-permute-start | bytes 786440 | tf_op jit(solution)/shard_map/ppermute | solution.py:23
  20.2 39.1 %copy-start.19 = (pred[256]{0:T(512)(128)(4,1)}, pred[256]{0:T(512)(128)(4,1)S(1)}, u32[]{:S(2)}) copy-start(pred[256]{0:T(512)(128)(4,1)S(1)} %compare_and_fusion) | copy-start | bytes 772
  35.7 0.9 copy-start.25
  36.5 0.7 copy-start.26
  36.6 1.0 copy-start.12
  37.2 0.7 copy-start.36
  41.9 0.9 copy-start.7
  43.1 0.7 copy-start.31
  43.8 0.9 copy-start.28
  43.8 1.1 copy-start.40
  61.3 1.5 copy-start.20
  70.0 8.4 %collective-permute-start.3 = (bf16[4,8,8,512]{3,2,1,0:T(8,128)(2,1)S(1)}, bf16[4,8,8,512]{3,2,1,0:T(8,128)(2,1)S(1)}, u32[]{:S(2)}, u32[]{:S(2)}) collective-permute-start(bf16[4,8,8,512]{3,2,1,0:T(8,128)(2,1)S(1)} %split.34), channel_id=1, source_target_pairs={{0,1},{1,2},{2,3},{3,4},{4,5},{5,6},{6,7},{7,8},{8,9},{9,10},{10,1... | collective-permute-start | bytes 786440 | tf_op jit(solution)/shard_map/ppermute | solution.py:23
  72.6 0.9 copy-start.3
  72.6 1.0 copy-start.18
  73.6 0.9 copy-start.17
  74.5 0.9 copy-start.16
  75.6 0.9 copy-start.9
  75.6 8.2 %collective-permute-start.2 = (bf16[4,8,8,512]{3,2,1,0:T(8,128)(2,1)S(1)}, bf16[4,8,8,512]{3,2,1,0:T(8,128)(2,1)S(1)}, u32[]{:S(2)}, u32[]{:S(2)}) collective-permute-start(bf16[4,8,8,512]{3,2,1,0:T(8,128)(2,1)S(1)} %split.35), channel_id=1, source_target_pairs={{0,16},{16,32},{32,48},{48,64},{64,80},{80,96},{96,112},{112,128},... | collective-permute-start | bytes 786440 | tf_op jit(solution)/shard_map/ppermute | solution.py:23
  76.5 0.9 copy-start.27
  77.4 6.4 %copy-start.13 = (f32[4,8,8,256]{3,2,1,0:T(8,128)S(1)}, f32[4,8,8,256]{3,2,1,0:T(8,128)}, u32[]{:S(2)}) copy-start(f32[4,8,8,256]{3,2,1,0:T(8,128)} %get-tuple-element.105) | copy-start | bytes 786436
  85.1 1.4 copy-start.11
  85.1 0.7 copy-start.39
  85.9 0.7 copy-start.37
  86.5 1.0 copy-start.5
  86.6 1.0 copy-start.34
  87.5 0.7 copy-start.24
  88.2 0.7 copy-start.22
  89.1 0.7 copy-start.30
  352.8 1.7 copy-start.8
  354.5 1.1 copy-start.15
  354.5 1.8 copy-start.6
  356.3 1.1 copy-start.14
  356.3 1.8 copy-start.2
  358.1 1.6 copy-start.1
Sparse Core Ops, SparseCore 0:
  85.3 267.4 all-reduce.50
where the time goes:
time: 369 us; the launch traced here: 368 us
  waiting for transfers between devices  192 us (52%)
  blocking collectives  76.5 us (21%)
  matrix products  32.2 us (9%)
  between operations  26.4 us (7%)
  local copies, waits for them, and re-layouts  23.1 us (6%)
  starting transfers between devices  11.2 us (3%)
  other arithmetic  6.54 us (2%)
    psum x1, waiting for transfers between devices, on_device(): lax.psum((grad_flip * scale, plan_step_gradient * scale, grad_gain_tanner...  186 us
    psum x1, blocking collectives, on_device(): lax.psum((grad_flip * scale, plan_step_gradient * scale, grad_gain_tanner...  76.5 us
    unnamed x89, local copies, waits for them, and re-layouts  19.3 us
    dot_general x34, matrix products, head_total(): lax.dot_general(product, block, (((product.ndim - 1,), (0,)), ((), ())),...  15.4 us
    ppermute x4, starting transfers between devices, shifted(): return lax.ppermute(x, axis, [(i, (i + by) % count) for i in range(count)])  11.1 us
    dot_general x7, matrix products, back_matmul(): lax.dot_general(flat_inputs, flat_grad, (((0,), (0,)), ((), ())), preferr...  8.03 us
  transfers between devices with their start and end apart: 5, of which 2 were waited for; matrix products, arithmetic and copies ran while one was open for 1% of the time, Pallas kernels for 0%

commit v1 on v0

--- a/solution.py
+++ b/solution.py
@@ -3,6 +3,8 @@
 import jax
 import jax.numpy as jnp
 from jax import lax
+from jax.experimental import pallas as pl
+from jax.experimental.pallas import tpu as pltpu
 from jax.sharding import PartitionSpec as P
 
 MODEL_WIDTH = 256
@@ -16,6 +18,307 @@
 CAP = 4.0
 EXACT_PRECISION = lax.Precision.HIGHEST
 ALONG_ROWS = (0, 4, 5)
+
+
+MESH = pl.DeviceIdType.MESH
+GROUP_ROWS = 4096
+HALF = 2048
+SMALL_ROWS = 16
+
+
+class Place:
+    def __init__(self):
+        self.gx = lax.axis_index("gx")
+        self.gy = lax.axis_index("gy")
+        self.z = lax.rem(self.gx, 8)
+        self.y_lo = lax.div(self.gx, 8)
+        self.core = lax.rem(self.gy, 2)
+        self.y_hi = lax.rem(lax.div(self.gy, 2), 2)
+        self.x = lax.div(self.gy, 4)
+        self.y = self.y_hi * 2 + self.y_lo
+
+    def other_core(self):
+        return (self.gx, self.gy + 1 - 2 * self.core)
+
+    def at_x(self, x):
+        return (self.gx, x * 4 + self.y_hi * 2 + self.core)
+
+    def at_y(self, y):
+        return (lax.rem(y, 2) * 8 + self.z, self.x * 4 + lax.div(y, 2) * 2 + self.core)
+
+    def at_z(self, z):
+        return (self.y_lo * 8 + z, self.gy)
+
+    def greeted(self):
+        peers = [self.other_core()]
+        for step in range(1, 4):
+            peers.append(self.at_x(lax.rem(self.x + step, 4)))
+            peers.append(self.at_y(lax.rem(self.y + step, 4)))
+        for step in range(1, 8):
+            peers.append(self.at_z(lax.rem(self.z + step, 8)))
+        return peers
+
+
+def greet(peers):
+    barrier = pltpu.get_barrier_semaphore()
+    for peer in peers:
+        pl.semaphore_signal(barrier, inc=1, device_id=peer, device_id_type=MESH)
+    return barrier, len(peers)
+
+
+def rows(start, count):
+    return pl.ds(pl.multiple_of(start, 16), count)
+
+
+class Sum:
+    SCRATCH = (
+        pltpu.VMEM((HALF, 128), jnp.bfloat16),
+        pltpu.VMEM((HALF, 128), jnp.bfloat16),
+        pltpu.VMEM((6, 256, 128), jnp.bfloat16),
+        pltpu.VMEM((2, 256, 128), jnp.bfloat16),
+        pltpu.VMEM((6, 64, 128), jnp.bfloat16),
+        pltpu.VMEM((128, 128), jnp.bfloat16),
+        pltpu.VMEM((7, 16, 128), jnp.bfloat16),
+        pltpu.SemaphoreType.DMA((40,)),
+        pltpu.SemaphoreType.DMA((40,)),
+    )
+
+    def __init__(self, place, group, source, result, scratch):
+        self.place = place
+        self.source = source
+        self.base = group * GROUP_ROWS
+        self.result = result
+        (self.from_core, self.one, self.in_two, self.two, self.in_three, self.three, self.in_four,
+         self.send, self.recv) = scratch
+
+    def copy(self, slot, source, target, peer):
+        copy = pltpu.make_async_remote_copy(
+            src_ref=source,
+            dst_ref=target,
+            send_sem=self.send.at[slot],
+            recv_sem=self.recv.at[slot],
+            device_id=peer,
+            device_id_type=MESH,
+        )
+        copy.start()
+        return copy
+
+    def core_out(self):
+        other = rows((1 - self.place.core) * HALF, HALF)
+        self.core_copy = self.copy(0, self.source.at[other], self.from_core, self.place.other_core())
+
+    def core_in(self):
+        p = self.place
+        self.core_copy.wait()
+        own = self.source[rows(p.core * HALF, HALF)]
+        self.one[...] = (own.astype(jnp.float32) + self.from_core[...].astype(jnp.float32)).astype(jnp.bfloat16)
+        self.copies = []
+        for step in range(1, 4):
+            x, y = lax.rem(p.x + step, 4), lax.rem(p.y + step, 4)
+            self.copies.append(
+                self.copy(step, self.one.at[rows(x * 256, 256)], self.in_two.at[step - 1], p.at_x(x)))
+            self.copies.append(
+                self.copy(3 + step, self.one.at[rows(1024 + y * 256, 256)], self.in_two.at[2 + step], p.at_y(y)))
+
+    def two_in(self):
+        p = self.place
+        for copy in self.copies:
+            copy.wait()
+        for part, own in ((0, p.x * 256), (1, 1024 + p.y * 256)):
+            total = self.one[rows(own, 256)].astype(jnp.float32)
+            for step in range(3):
+                total = total + self.in_two[part * 3 + step].astype(jnp.float32)
+            self.two[part] = total.astype(jnp.bfloat16)
+        self.copies = []
+        for step in range(1, 4):
+            x, y = lax.rem(p.x + step, 4), lax.rem(p.y + step, 4)
+            self.copies.append(
+                self.copy(6 + step, self.two.at[0, rows(y * 64, 64)], self.in_three.at[step - 1], p.at_y(y)))
+            self.copies.append(
+                self.copy(9 + step, self.two.at[1, rows(x * 64, 64)], self.in_three.at[2 + step], p.at_x(x)))
+
+    def three_in(self):
+        p = self.place
+        for copy in self.copies:
+            copy.wait()
+        for part, own in ((0, p.y * 64), (1, p.x * 64)):
+            total = self.two[part, rows(own, 64)].astype(jnp.float32)
+            for step in range(3):
+                total = total + self.in_three[part * 3 + step].astype(jnp.float32)
+            self.three[part * 64 : part * 64 + 64] = total.astype(jnp.bfloat16)
+        self.copies = []
+        for step in range(1, 8):
+            z = lax.rem(p.z + step, 8)
+            self.copies.append(
+                self.copy(12 + step, self.three.at[rows(z * 16, 16)], self.in_four.at[step - 1], p.at_z(z)))
+
+    def four_in(self):
+        p = self.place
+        for copy in self.copies:
+            copy.wait()
+        total = self.three[rows(p.z * 16, 16)].astype(jnp.float32)
+        for step in range(7):
+            total = total + self.in_four[step].astype(jnp.float32)
+        half = self.base + p.core * HALF
+        self.first = half + p.x * 256 + p.y * 64
+        self.second = half + 1024 + p.y * 256 + p.x * 64
+        upper = lax.div(p.z, 4)
+        own = (1 - upper) * self.first + upper * self.second + lax.rem(p.z, 4) * 16
+        self.result[rows(own, 16)] = total.astype(jnp.bfloat16)
+        self.copies = []
+        for step in range(1, 8):
+            z = lax.rem(p.z + step, 8)
+            tile = self.result.at[rows(own, 16)]
+            self.copies.append(self.copy(19 + step, tile, tile, p.at_z(z)))
+
+    def z_gathered(self):
+        p = self.place
+        for copy in self.copies:
+            copy.wait()
+        first, second = self.result.at[rows(self.first, 64)], self.result.at[rows(self.second, 64)]
+        self.copies = []
+        for step in range(1, 4):
+            x, y = lax.rem(p.x + step, 4), lax.rem(p.y + step, 4)
+            self.copies.append(self.copy(26 + step, first, first, p.at_y(y)))
+            self.copies.append(self.copy(29 + step, second, second, p.at_x(x)))
+
+    def one_gathered(self):
+        p = self.place
+        for copy in self.copies:
+            copy.wait()
+        half = self.base + p.core * HALF
+        first = self.result.at[rows(half + p.x * 256, 256)]
+        second = self.result.at[rows(half + 1024 + p.y * 256, 256)]
+        self.copies = []
+        for step in range(1, 4):
+            x, y = lax.rem(p.x + step, 4), lax.rem(p.y + step, 4)
+            self.copies.append(self.copy(32 + step, first, first, p.at_x(x)))
+            self.copies.append(self.copy(35 + step, second, second, p.at_y(y)))
+
+    def both_gathered(self):
+        p = self.place
+        for copy in self.copies:
+            copy.wait()
+        own = self.result.at[rows(self.base + p.core * HALF, HALF)]
+        self.core_copy = self.copy(39, own, own, p.other_core())
+
+    def finish(self):
+        self.core_copy.wait()
+
+
+class SmallSum:
+    SCRATCH = (
+        pltpu.VMEM((2, SMALL_ROWS, 256), jnp.float32),
+        pltpu.VMEM((4, SMALL_ROWS, 256), jnp.float32),
+        pltpu.VMEM((4, SMALL_ROWS, 256), jnp.float32),
+        pltpu.VMEM((8, SMALL_ROWS, 256), jnp.float32),
+        pltpu.SemaphoreType.DMA((14,)),
+        pltpu.SemaphoreType.DMA((14,)),
+    )
+
+    def __init__(self, place, scratch):
+        self.place = place
+        self.slots = scratch[:4]
+        self.send, self.recv = scratch[4:]
+        self.stage = -1
+
+    def out(self, value):
+        p = self.place
+        self.stage += 1
+        slots = self.slots[self.stage]
+        mine = (p.core, p.x, p.y, p.z)[self.stage]
+        at = (lambda _: p.other_core(), p.at_x, p.at_y, p.at_z)[self.stage]
+        first = (0, 1, 4, 7)[self.stage]
+        count = slots.shape[0]
+        slots[mine] = value
+        self.copies = []
+        for step in range(1, count):
+            copy = pltpu.make_async_remote_copy(
+                src_ref=slots.at[mine],
+                dst_ref=slots.at[mine],
+                send_sem=self.send.at[first + step - 1],
+                recv_sem=self.recv.at[first + step - 1],
+                device_id=at(lax.rem(mine + step, count)),
+                device_id_type=MESH,
+            )
+            copy.start()
+            self.copies.append(copy)
+
+    def total(self):
+        for copy in self.copies:
+            copy.wait()
+        slots = self.slots[self.stage]
+        total = slots[0]
+        for index in range(1, slots.shape[0]):
+            total = total + slots[index]
+        return total
+
+
+def sum_kernel(early_ref, late_ref, small_ref, result_ref, small_result_ref, *scratch):
+    place = Place()
+    barrier, count = greet(place.greeted())
+    pl.semaphore_wait(barrier, count)
+    per = len(Sum.SCRATCH)
+    early = Sum(place, 0, early_ref, result_ref, scratch[:per])
+    late = Sum(place, 1, late_ref, result_ref, scratch[per : 2 * per])
+    small = SmallSum(place, scratch[2 * per :])
+    early.core_out()
+    late.core_out()
+    small.out(small_ref[...])
+    early.core_in()
+    late.core_in()
+    small.out(small.total())
+    early.two_in()
+    late.two_in()
+    small.out(small.total())
+    early.three_in()
+    late.three_in()
+    small.out(small.total())
+    early.four_in()
+    late.four_in()
+    small_result_ref[...] = small.total()
+    early.z_gathered()
+    late.z_gathered()
+    early.one_gathered()
+    late.one_gathered()
+    early.both_gathered()
+    late.both_gathered()
+    early.finish()
+    late.finish()
+
+
+def sum_everywhere(early, late, small):
+    vmem = pl.BlockSpec(memory_space=pltpu.VMEM)
+    return pl.pallas_call(
+        sum_kernel,
+        out_shape=(
+            jax.ShapeDtypeStruct((2 * GROUP_ROWS, 128), jnp.bfloat16),
+            jax.ShapeDtypeStruct((SMALL_ROWS, 256), jnp.float32),
+        ),
+        in_specs=[vmem] * 3,
+        out_specs=(vmem, vmem),
+        scratch_shapes=list(Sum.SCRATCH + Sum.SCRATCH + SmallSum.SCRATCH),
+        compiler_params=pltpu.CompilerParams(
+            collective_id=0, has_side_effects=True, vmem_limit_bytes=40 * 2**20),
+    )(early, late, small)
+
+
+def to_slabs(*grads):
+    slabs = []
+    for grad in grads:
+        blocks, columns = grad.shape[0] // 256, grad.shape[1] // 128
+        slabs.append(grad.reshape(blocks, 256, columns, 128).transpose(0, 2, 1, 3).reshape(-1, 128))
+    return jnp.concatenate(slabs).astype(jnp.bfloat16)
+
+
+def from_slabs(slabs, scale, *shapes):
+    grads, at = [], 0
+    for depth, width in shapes:
+        count = depth * width // 128
+        piece = slabs[at : at + count].reshape(depth // 256, width // 128, 256, 128).transpose(0, 2, 1, 3)
+        grads.append(piece.reshape(depth, width).astype(jnp.float32) * scale)
+        at += count
+    return grads
 
 
 def shifted(x, axis, by):
@@ -203,37 +506,45 @@
         (((0,), (0,)), ((), ())),
         precision=EXACT_PRECISION,
     )
-    summed = lax.psum(
-        (
-            grad_flip * scale,
-            plan_step_gradient * scale,
-            grad_gain_tanner * scale,
-            grad_query * scale,
-            grad_key_value * scale,
-            grad_merge * scale,
-            grad_gain_time * scale,
-            grad_temporal * scale,
-            grad_temporal_out * scale,
-            grad_gain_ffn * scale,
-            grad_up * scale,
-            grad_down * scale,
-        ),
-        ("gx", "gy"),
-    )
+    small = jnp.concatenate(
+        [
+            grad_flip[None],
+            plan_step_gradient,
+            grad_gain_tanner[None],
+            grad_gain_time[None],
+            grad_gain_ffn[None],
+            jnp.zeros((SMALL_ROWS - 12, MODEL_WIDTH), jnp.float32),
+        ]
+    )
+    early = to_slabs(grad_down, grad_up)
+    late = to_slabs(grad_query, grad_key_value, grad_merge, grad_temporal, grad_temporal_out)
+    slabs, small = sum_everywhere(early, late, small)
+    down, up, query_g, key_value_g, merge_g, temporal_g, temporal_out_g = from_slabs(
+        slabs,
+        scale,
+        (1024, 256),
+        (256, 1024),
+        (256, 256),
+        (256, 512),
+        (256, 256),
+        (256, 768),
+        (256, 256),
+    )
+    small = small * scale
     return (
         token_grad,
-        summed[0],
-        summed[1],
-        summed[2],
-        summed[3],
-        summed[4],
-        summed[5],
-        summed[6],
-        summed[7],
-        summed[8],
-        summed[9],
-        summed[10],
-        summed[11],
+        small[0],
+        small[1:9],
+        small[9],
+        query_g,
+        key_value_g,
+        merge_g,
+        small[10],
+        temporal_g,
+        temporal_out_g,
+        small[11],
+        up,
+        down,
     )
 
 

time: 369 us -> 142 us (0.38)
  waiting for transfers between devices: 192 us -> 0.01 us
  blocking collectives: 76.5 us -> 0 us
  Pallas kernels: 0 us -> 44 us
  between operations: 26.4 us -> 13.6 us
  other arithmetic: 6.54 us -> 13 us
    psum x1 -> x0, waiting for transfers between devices: 186 us -> none  [on_device(): lax.psum((grad_flip * scale, plan_step_gradient * scale, grad_gain_tanner...]
    psum x1 -> x0, blocking collectives: 76.5 us -> none  [on_device(): lax.psum((grad_flip * scale, plan_step_gradient * scale, grad_gain_tanner...]
    pallas_call x0 -> x1, Pallas kernels: none -> 44 us  [sum_everywhere(): pl.pallas_call(sum_kernel, out_shape=(jax.ShapeDtypeStruct((2 * GROUP_ROW...]
    unnamed x89 -> x119, local copies, waits for them, and re-layouts: 19.3 us -> 9.73 us
    dot_general x0 -> x8, local copies, waits for them, and re-layouts: none -> 5.81 us  [back_matmul(): lax.dot_general(flat_inputs, flat_grad, (((0,), (0,)), ((), ())), preferr...]
    ppermute x4, waiting for transfers between devices: 5.5 us -> 0.01 us  [shifted(): return lax.ppermute(x, axis, [(i, (i + by) % count) for i in range(count)])]
  transfers between devices with their start and end apart: 5 -> 4, of which waited for: 2 -> 0; matrix products, arithmetic and copies ran while one was open for 1% -> 11% of each run, Pallas kernels for 0% -> 0%
where the time goes in v1:
time: 142 us; the launch traced here: 141 us
  Pallas kernels  44 us (31%)
  matrix products  34.3 us (24%)
  local copies, waits for them, and re-layouts  25.4 us (18%)
  between operations  13.6 us (10%)
  other arithmetic  13 us (9%)
  starting transfers between devices  11 us (8%)
    pallas_call x1, Pallas kernels, sum_everywhere(): pl.pallas_call(sum_kernel, out_shape=(jax.ShapeDtypeStruct((2 * GROUP_ROW...  44 us
    dot_general x34, matrix products, head_total(): lax.dot_general(product, block, (((product.ndim - 1,), (0,)), ((), ())),...  15.5 us
    ppermute x4, starting transfers between devices, shifted(): return lax.ppermute(x, axis, [(i, (i + by) % count) for i in range(count)])  11 us
    unnamed x119, local copies, waits for them, and re-layouts  9.73 us
    dot_general x7, matrix products, back_matmul(): lax.dot_general(flat_inputs, flat_grad, (((0,), (0,)), ((), ())), preferr...  6.87 us
    dot_general x7, matrix products, back_matmul(): lax.dot_general(grad_low, weight, (((grad_low.ndim - 1,), (1,)), ((), ())...  6.76 us
    dot_general x8, local copies, waits for them, and re-layouts, back_matmul(): lax.dot_general(flat_inputs, flat_grad, (((0,), (0,)), ((), ())), preferr...  5.81 us
    dot_general x6, matrix products, matmul(): lax.dot_general(inputs, weight, (((inputs.ndim - 1,), (0,)), ((), ())), p...  3.51 us
  transfers between devices with their start and end apart: 4, of which 0 were waited for; matrix products, arithmetic and copies ran while one was open for 11% of the time, Pallas kernels for 0%

profile of v1, /device:TPU:1, one launch (start us, length us, event | category | flops | bytes accessed | tf_op | source)
XLA Modules:
  0.0 141.3 jit_solution(10662672178314620907)
XLA Ops:
  0.7 0.8 convert_element_type.151
  1.5 1.4 multiply_reduce_fusion.9
  2.9 0.8 multiply_convert_fusion.3
  3.7 1.2 fusion.469
  4.9 7.5 %collective-permute-start = (bf16[4,8,8,512]{3,2,1,0:T(8,128)(2,1)S(1)}, bf16[4,8,8,512]{3,2,1,0:T(8,128)(2,1)S(1)}, u32[]{:S(2)}, u32[]{:S(2)}) collective-permute-start(bf16[4,8,8,512]{3,2,1,0:T(8,128)(2,1)S(1)} %get-tuple-element.179), channel_id=1, source_target_pairs={{0,240},{16,0},{32,16},{48,32},{64,48},{80,64},{96,80},{112,96},{1... | collective-permute-start | bytes 786440 | tf_op jit(solution)/shard_map/ppermute | solution.py:326
  12.4 1.0 collective-permute-start.1
  21.8 0.7 copy.54
  26.8 0.8 fusion.30
  30.2 0.8 add_convert_fusion.2
  36.4 1.3 multiply_convert_fusion
  37.7 0.9 fusion.25
  38.6 0.9 multiply_reduce_fusion
  44.4 1.1 multiply_reduce_fusion.1
  45.5 0.9 fusion.462
  46.4 1.9 %fusion.451 = (f32[4,8,8,256]{3,2,1,0:T(8,128)}, f32[4,8,8,256]{3,2,1,0:T(8,128)S(1)}, f32[4,8,8,256]{3,2,1,0:T(8,128)}, f32[4,8,8,256]{3,2,1,0:T(8,128)}, f32[4...) fusion(f32[4,8,8,256]{3,2,1,0:T(8,128)S(1)} %get-tuple-element., ...), kind=kOutput, calls=%fused_computation.626 | convolution fusion | flops 37289984 | bytes 6553600 | tf_op jit(solution)/shard_map/dot_general | solution.py:341
  52.1 1.7 %fusion.466 = (f32[4,8,8,256]{3,2,1,0:T(8,128)}, bf16[4,8,8,256]{3,2,1,0:T(8,128)(2,1)S(1)}, f32[4,8,8,256]{3,2,1,0:T(8,128)S(1)}, f32[4,8,8,256]{3,2,1,0:T(8,12...) fusion(f32[4,8,8,256]{3,2,1,0:T(8,128)S(1)} %fusion.8, ...), kind=kOutput, calls=%fused_computation.634 | convolution fusion | flops 203620352 | bytes 6951936 | tf_op jit(solution)/shard_map/transpose(jvp())/dot_general | solution.py:360
  54.0 0.9 dynamic_update_slice.22
  54.9 1.1 add_add_fusion.1
  56.0 1.0 add_any.332
  57.1 1.2 add_add_fusion
  58.3 1.0 add_any.335
  59.3 0.7 split.34
  60.1 2.5 %collective-permute-start.3 = (bf16[4,8,8,512]{3,2,1,0:T(8,128)(2,1)}, bf16[4,8,8,512]{3,2,1,0:T(8,128)(2,1)}, u32[]{:S(2)}, u32[]{:S(2)}) collective-permute-start(bf16[4,8,8,512]{3,2,1,0:T(8,128)(2,1)} %split.34), channel_id=1, source_target_pairs={{0,1},{1,2},{2,3},{3,4},{4,5},{5,6},{6,7},{7,8},{8,9},{9,10},{10,1... | collective-permute-start | bytes 786440 | tf_op jit(solution)/shard_map/ppermute | solution.py:326
  62.7 1.0 add_dynamic-update-slice_fusion.2
  64.0 1.0 copy-done.1
  65.7 0.9 fusion.184
  66.7 0.8 copy.65
  67.4 0.7 copy.57
  68.2 1.0 copy.61
  69.4 1.2 copy.53
  70.7 0.9 convolution_convert_fusion.6
  71.6 1.1 convolution_convert_fusion.8
  72.7 0.9 convolution_convert_fusion.7
  74.0 1.3 convolution_convert_fusion.1
  75.4 0.9 copy.63
  76.3 2.1 %convolution_convert_fusion.2 = bf16[256,6,128]{2,0,1:T(8,128)(2,1)} fusion(bf16[256,256,1]{1,0,2:T(8,128)(2,1)S(1)} %bitcast.757, bf16[6,128,256]{2,1,0:T(8,128)(2,1)} %bitcast.756), kind=kOutput, calls=%fused_computation.16 | convolution fusion | flops 100859904 | bytes 917504 | tf_op jit(solution)/shard_map/dot_general | solution.py:349
  78.4 1.8 %fusion.34 = bf16[4,8,8,512]{3,2,1,0:T(8,128)(2,1)S(1)} fusion(f32[4,16,8,512]{3,2,1,0:T(8,128)} %copy-done.1, f32[4,8,16,512]{3,2,1,0:T(8,128)} %copy-done.2, bf16[4,8,8,512]{3,2,1,0:T(8,128)(2,1)} %collective-permute-done.3, bf16[4,8,8,512]{3,2,1,0:T(8,128)(2,1)} %collective-permute-done.2, f32[4,8,8,256]{3,2,1,0:T(8,128)} %get-tuple-element.154, ...), kind=kLoop, calls=%fused_computation.92 | loop fusion | flops 1048576 | bytes 2359296 | tf_op jit(solution)/shard_map/convert_element_type | solution.py:340
  80.3 0.8 multiply_reduce_fusion.2
  81.2 0.8 multiply_reduce_fusion.3
  83.5 1.0 constant_dynamic-update-slice_fusion.1
  84.6 0.8 concatenate.25.small_ref
  85.4 44.0 %shard_map.274 = (bf16[8192,128]{1,0:T(8,128)(2,1)S(1)}, f32[16,256]{1,0:T(8,128)S(1)}) custom-call(bf16[4096,128]{1,0:T(8,128)(2,1)S(1)} %pad_maximum_fusion.early_ref, bf16[4096,128]{1,0:T(8,128)(2,1)S(1)} %constant_dynamic-update-slice_fusion.late_ref, f32[16,256]{1,0:T(8,128)S(1)} %concatenate.25.small_ref), custom_call_target="tpu_custom_call" | custom-call | tf_op jit(solution)/shard_map/pallas_call | solution.py:292
  129.7 0.8 convert_multiply_fusion.4
  132.3 0.8 copy.73
  133.1 1.0 copy.111
  134.7 1.2 copy.112
  136.2 1.1 copy.74
  137.7 0.8 copy.113
  (205 shorter events, 26.6 us)
Async XLA Ops:
  0.6 35.8 %copy-start = (bf16[256,1024]{1,0:T(8,128)(2,1)S(1)}, bf16[256,1024]{1,0:T(8,128)(2,1)}, u32[]{:S(2)}) copy-start(bf16[256,1024]{1,0:T(8,128)(2,1)} %param.39) | copy-start | bytes 1572868
  0.7 12.7 %copy-start.46 = (s32[6,2]{0,1:T(2,128)S(1)}, s32[6,2]{0,1:T(2,128)}, u32[]{:S(2)}) copy-start(s32[6,2]{0,1:T(2,128)} %param.28) | copy-start | bytes 148
  0.7 21.1 %copy-start.12 = (bf16[4,8,8,256]{3,2,1,0:T(8,128)(2,1)S(1)}, bf16[4,8,8,256]{3,2,1,0:T(8,128)(2,1)}, u32[]{:S(2)}) copy-start(bf16[4,8,8,256]{3,2,1,0:T(8,128)(2,1)} %param.41) | copy-start | bytes 393220
  0.7 25.7 %copy-start.33 = (bf16[256,256]{1,0:T(8,128)(2,1)S(1)}, bf16[256,256]{1,0:T(8,128)(2,1)}, u32[]{:S(2)}) copy-start(bf16[256,256]{1,0:T(8,128)(2,1)} %param.32) | copy-start | bytes 393220
  2.9 22.9 %copy-start.41 = (f32[4,8,8]{2,1,0:T(8,128)}, f32[4,8,8]{2,1,0:T(8,128)S(1)}, u32[]{:S(2)}) copy-start(f32[4,8,8]{2,1,0:T(8,128)S(1)} %get-tuple-element.176) | copy-start | bytes 3076
  2.9 22.9 %copy-start.35 = (f32[4,8,8]{2,1,0:T(8,128)}, f32[4,8,8]{2,1,0:T(8,128)S(1)}, u32[]{:S(2)}) copy-start(f32[4,8,8]{2,1,0:T(8,128)S(1)} %fusion.395) | copy-start | bytes 3076
  3.7 67.9 %copy-start.3 = (bf16[4,8,8,256]{3,2,1,0:T(8,128)(2,1)}, bf16[4,8,8,256]{3,2,1,0:T(8,128)(2,1)S(1)}, u32[]{:S(2)}) copy-start(bf16[4,8,8,256]{3,2,1,0:T(8,128)(2,1)S(1)} %multiply_convert_fusion.3) | copy-start | bytes 393220
  4.9 21.7 %collective-permute-start = (bf16[4,8,8,512]{3,2,1,0:T(8,128)(2,1)S(1)}, bf16[4,8,8,512]{3,2,1,0:T(8,128)(2,1)S(1)}, u32[]{:S(2)}, u32[]{:S(2)}) collective-permute-start(bf16[4,8,8,512]{3,2,1,0:T(8,128)(2,1)S(1)} %get-tuple-element.179), channel_id=1, source_target_pairs={{0,240},{16,0},{32,16},{48,32},{64,48},{80,64},{96,80},{112,96},{1... | collective-permute-start | bytes 786440 | tf_op jit(solution)/shard_map/ppermute | solution.py:326
  12.4 14.3 %collective-permute-start.1 = (bf16[4,8,8,512]{3,2,1,0:T(8,128)(2,1)S(1)}, bf16[4,8,8,512]{3,2,1,0:T(8,128)(2,1)S(1)}, u32[]{:S(2)}, u32[]{:S(2)}) collective-permute-start(bf16[4,8,8,512]{3,2,1,0:T(8,128)(2,1)S(1)} %get-tuple-element.179), channel_id=1, source_target_pairs={{0,15},{1,0},{2,1},{3,2},{4,3},{5,4},{6,5},{7,6},{8,7},{9,8},{10,9... | collective-permute-start | bytes 786440 | tf_op jit(solution)/shard_map/ppermute | solution.py:326
  30.2 1.5 %copy-start.47 = (f32[256]{0:T(256)S(1)}, f32[256]{0:T(256)}, u32[]{:S(2)}) copy-start(f32[256]{0:T(256)} %param.35) | copy-start | bytes 3076
  30.2 1.6 %copy-start.9 = (bf16[256,768]{1,0:T(8,128)(2,1)S(1)}, bf16[256,768]{1,0:T(8,128)(2,1)}, u32[]{:S(2)}) copy-start(bf16[256,768]{1,0:T(8,128)(2,1)} %param.36) | copy-start | bytes 1179652
  31.8 2.8 %copy-start.10 = (bf16[4,8,8,256]{3,2,1,0:T(8,128)(2,1)}, bf16[4,8,8,256]{3,2,1,0:T(8,128)(2,1)S(1)}, u32[]{:S(2)}) copy-start(bf16[4,8,8,256]{3,2,1,0:T(8,128)(2,1)S(1)} %multiply_convert_fusion.2) | copy-start | bytes 393220
  33.6 2.4 %copy-start.32 = (bf16[256,256]{1,0:T(8,128)(2,1)S(1)}, bf16[256,256]{1,0:T(8,128)(2,1)}, u32[]{:S(2)}) copy-start(bf16[256,256]{1,0:T(8,128)(2,1)} %param.37) | copy-start | bytes 393220
  33.9 2.3 %copy-start.45 = (f32[256]{0:T(256)S(1)}, f32[256]{0:T(256)}, u32[]{:S(2)}) copy-start(f32[256]{0:T(256)} %param.38) | copy-start | bytes 3076
  36.0 1.8 %copy-start.53 = (bf16[1024,256]{1,0:T(8,128)(2,1)S(1)}, bf16[1024,256]{1,0:T(8,128)(2,1)}, u32[]{:S(2)}) copy-start(bf16[1024,256]{1,0:T(8,128)(2,1)} %param.40) | copy-start | bytes 1572868
  46.4 1.9 %copy-start.27 = (bf16[4,8,8,256]{3,2,1,0:T(8,128)(2,1)}, bf16[4,8,8,256]{3,2,1,0:T(8,128)(2,1)S(1)}, u32[]{:S(2)}) copy-start(bf16[4,8,8,256]{3,2,1,0:T(8,128)(2,1)S(1)} %get-tuple-element.78) | copy-start | bytes 393220
  57.0 5.7 %copy-start.18 = (f32[4,8,8,256]{3,2,1,0:T(8,128)S(1)}, f32[4,8,8,256]{3,2,1,0:T(8,128)}, u32[]{:S(2)}) copy-start(f32[4,8,8,256]{3,2,1,0:T(8,128)} %get-tuple-element.158) | copy-start | bytes 786436
  59.3 4.6 %copy-start.2 = (f32[4,8,16,512]{3,2,1,0:T(8,128)}, f32[4,8,16,512]{3,2,1,0:T(8,128)S(1)}, u32[]{:S(2)}) copy-start(f32[4,8,16,512]{3,2,1,0:T(8,128)S(1)} %add_any.335) | copy-start | bytes 3145732
  59.3 4.4 %copy-start.17 = (f32[4,8,8,256]{3,2,1,0:T(8,128)S(1)}, f32[4,8,8,256]{3,2,1,0:T(8,128)}, u32[]{:S(2)}) copy-start(f32[4,8,8,256]{3,2,1,0:T(8,128)} %get-tuple-element.157) | copy-start | bytes 786436
  59.3 4.4 %copy-start.38 = (f32[4,8,8,256]{3,2,1,0:T(8,128)S(1)}, f32[4,8,8,256]{3,2,1,0:T(8,128)}, u32[]{:S(2)}) copy-start(f32[4,8,8,256]{3,2,1,0:T(8,128)} %get-tuple-element.120) | copy-start | bytes 786436
  59.3 4.6 %copy-start.37 = (f32[4,8,8,256]{3,2,1,0:T(8,128)S(1)}, f32[4,8,8,256]{3,2,1,0:T(8,128)}, u32[]{:S(2)}) copy-start(f32[4,8,8,256]{3,2,1,0:T(8,128)} %get-tuple-element.119) | copy-start | bytes 786436
  60.1 18.3 %collective-permute-start.3 = (bf16[4,8,8,512]{3,2,1,0:T(8,128)(2,1)}, bf16[4,8,8,512]{3,2,1,0:T(8,128)(2,1)}, u32[]{:S(2)}, u32[]{:S(2)}) collective-permute-start(bf16[4,8,8,512]{3,2,1,0:T(8,128)(2,1)} %split.34), channel_id=1, source_target_pairs={{0,1},{1,2},{2,3},{3,4},{4,5},{5,6},{6,7},{7,8},{8,9},{9,10},{10,1... | collective-permute-start | bytes 786440 | tf_op jit(solution)/shard_map/ppermute | solution.py:326
  63.7 2.0 %copy-start.34 = (bf16[256,256]{1,0:T(8,128)(2,1)S(1)}, bf16[256,256]{1,0:T(8,128)(2,1)}, u32[]{:S(2)}) copy-start(bf16[256,256]{1,0:T(8,128)(2,1)} %param.32) | copy-start | bytes 393220
  63.8 2.9 %copy-start.15 = (bf16[4,8,8,256]{3,2,1,0:T(8,128)(2,1)S(1)}, bf16[4,8,8,256]{3,2,1,0:T(8,128)(2,1)}, u32[]{:S(2)}) copy-start(bf16[4,8,8,256]{3,2,1,0:T(8,128)(2,1)} %copy-done.14) | copy-start | bytes 393220
  63.9 5.3 %copy-start.8 = (bf16[4,8,8,1024]{3,2,1,0:T(8,128)(2,1)S(1)}, bf16[4,8,8,1024]{3,2,1,0:T(8,128)(2,1)}, u32[]{:S(2)}) copy-start(bf16[4,8,8,1024]{3,2,1,0:T(8,128)(2,1)} %copy-done.7) | copy-start | bytes 1572868
  65.0 5.7 %copy-start.28 = (bf16[4,8,8,256]{3,2,1,0:T(8,128)(2,1)S(1)}, bf16[4,8,8,256]{3,2,1,0:T(8,128)(2,1)}, u32[]{:S(2)}) copy-start(bf16[4,8,8,256]{3,2,1,0:T(8,128)(2,1)} %pad_maximum_fusion.1) | copy-start | bytes 393220
  65.7 12.7 %collective-permute-start.2 = (bf16[4,8,8,512]{3,2,1,0:T(8,128)(2,1)}, bf16[4,8,8,512]{3,2,1,0:T(8,128)(2,1)}, u32[]{:S(2)}, u32[]{:S(2)}) collective-permute-start(bf16[4,8,8,512]{3,2,1,0:T(8,128)(2,1)} %split.35), channel_id=1, source_target_pairs={{0,16},{16,32},{32,48},{48,64},{64,80},{80,96},{96,112},{112,128},... | collective-permute-start | bytes 786440 | tf_op jit(solution)/shard_map/ppermute | solution.py:326
  65.7 7.0 %copy-start.24 = (bf16[4,8,8,256]{3,2,1,0:T(8,128)(2,1)S(1)}, bf16[4,8,8,256]{3,2,1,0:T(8,128)(2,1)}, u32[]{:S(2)}) copy-start(bf16[4,8,8,256]{3,2,1,0:T(8,128)(2,1)} %copy-done.23) | copy-start | bytes 393220
  66.7 7.0 %copy-start.26 = (bf16[4,8,8,256]{3,2,1,0:T(8,128)(2,1)S(1)}, bf16[4,8,8,256]{3,2,1,0:T(8,128)(2,1)}, u32[]{:S(2)}) copy-start(bf16[4,8,8,256]{3,2,1,0:T(8,128)(2,1)} %copy-done.25) | copy-start | bytes 393220
  68.2 2.5 %copy-start.31 = (bf16[256,256]{1,0:T(8,128)(2,1)S(1)}, bf16[256,256]{1,0:T(8,128)(2,1)}, u32[]{:S(2)}) copy-start(bf16[256,256]{1,0:T(8,128)(2,1)} %copy.65) | copy-start | bytes 393220
  74.0 2.3 %copy-start.11 = (bf16[4,8,8,256]{3,2,1,0:T(8,128)(2,1)S(1)}, bf16[4,8,8,256]{3,2,1,0:T(8,128)(2,1)}, u32[]{:S(2)}) copy-start(bf16[4,8,8,256]{3,2,1,0:T(8,128)(2,1)} %copy-done.10) | copy-start | bytes 393220
  75.3 4.9 %copy-start.36 = (f32[4,8,8]{2,1,0:T(8,128)S(1)}, f32[4,8,8]{2,1,0:T(8,128)}, u32[]{:S(2)}) copy-start(f32[4,8,8]{2,1,0:T(8,128)} %copy-done.35) | copy-start | bytes 3076
  75.3 4.9 %copy-start.48 = (f32[256]{0:T(256)S(1)}, f32[256]{0:T(256)}, u32[]{:S(2)}) copy-start(f32[256]{0:T(256)} %param.31) | copy-start | bytes 3076
  76.3 3.9 %copy-start.20 = (f32[4,8,8,256]{3,2,1,0:T(8,128)S(1)}, f32[4,8,8,256]{3,2,1,0:T(8,128)}, u32[]{:S(2)}) copy-start(f32[4,8,8,256]{3,2,1,0:T(8,128)} %fusion.184) | copy-start | bytes 786436
  76.3 3.9 %copy-start.22 = (bf16[256,512]{1,0:T(8,128)(2,1)S(1)}, bf16[256,512]{1,0:T(8,128)(2,1)}, u32[]{:S(2)}) copy-start(bf16[256,512]{1,0:T(8,128)(2,1)} %param.33) | copy-start | bytes 786436
  76.3 4.8 %copy-start.42 = (f32[4,8,8]{2,1,0:T(8,128)S(1)}, f32[4,8,8]{2,1,0:T(8,128)}, u32[]{:S(2)}) copy-start(f32[4,8,8]{2,1,0:T(8,128)} %copy-done.41) | copy-start | bytes 3076
  78.4 2.7 %copy-start.16 = (f32[4,8,8,256]{3,2,1,0:T(8,128)S(1)}, f32[4,8,8,256]{3,2,1,0:T(8,128)}, u32[]{:S(2)}) copy-start(f32[4,8,8,256]{3,2,1,0:T(8,128)} %get-tuple-element.79) | copy-start | bytes 786436
  78.4 2.7 %copy-start.40 = (f32[4,8,8]{2,1,0:T(8,128)S(1)}, f32[4,8,8]{2,1,0:T(8,128)}, u32[]{:S(2)}) copy-start(f32[4,8,8]{2,1,0:T(8,128)} %copy-done.39) | copy-start | bytes 3076
  78.4 2.7 %copy-start.49 = (f32[256]{0:T(256)S(1)}, f32[256]{0:T(256)}, u32[]{:S(2)}) copy-start(f32[256]{0:T(256)} %param.31) | copy-start | bytes 3076
  78.4 4.2 %copy-start.44 = (s32[4,8,8]{2,1,0:T(8,128)S(1)}, s32[4,8,8]{2,1,0:T(8,128)}, u32[]{:S(2)}) copy-start(s32[4,8,8]{2,1,0:T(8,128)} %param.27) | copy-start | bytes 3076
  80.2 2.9 %copy-start.4 = (bf16[4,8,8,256]{3,2,1,0:T(8,128)(2,1)S(1)}, bf16[4,8,8,256]{3,2,1,0:T(8,128)(2,1)}, u32[]{:S(2)}) copy-start(bf16[4,8,8,256]{3,2,1,0:T(8,128)(2,1)} %copy-done.3) | copy-start | bytes 393220
  80.2 3.2 %copy-start.30 = (bf16[256,2,128]{2,0,1:T(8,128)(2,1)S(1)}, bf16[256,2,128]{2,0,1:T(8,128)(2,1)}, u32[]{:S(2)}) copy-start(bf16[256,2,128]{2,0,1:T(8,128)(2,1)} %convolution_convert_fusion.7) | copy-start | bytes 393220
  81.1 3.4 %copy-start.29 = (bf16[256,2,128]{2,0,1:T(8,128)(2,1)S(1)}, bf16[256,2,128]{2,0,1:T(8,128)(2,1)}, u32[]{:S(2)}) copy-start(bf16[256,2,128]{2,0,1:T(8,128)(2,1)} %convolution_convert_fusion.6) | copy-start | bytes 393220
  81.9 2.7 %copy-start.50 = (f32[256]{0:T(256)S(1)}, f32[256]{0:T(256)}, u32[]{:S(2)}) copy-start(f32[256]{0:T(256)} %get-tuple-element.70) | copy-start | bytes 3076
  81.9 2.7 %copy-start.51 = (f32[256]{0:T(256)S(1)}, f32[256]{0:T(256)}, u32[]{:S(2)}) copy-start(f32[256]{0:T(256)} %get-tuple-element.72) | copy-start | bytes 3076
  83.1 1.5 %copy-start.52 = (f32[256]{0:T(256)S(1)}, f32[256]{0:T(256)}, u32[]{:S(2)}) copy-start(f32[256]{0:T(256)} %get-tuple-element.76) | copy-start | bytes 3076
  129.5 2.1 %copy-start.6 = (f32[4,8,8,256]{3,2,1,0:T(8,128)S(1)}, f32[4,8,8,256]{3,2,1,0:T(8,128)}, u32[]{:S(2)}) copy-start(f32[4,8,8,256]{3,2,1,0:T(8,128)} %copy-done.5) | copy-start | bytes 786436
  136.2 2.3 %copy-start.21 = (f32[512,128]{1,0:T(8,128)S(1)}, f32[512,128]{1,0:T(8,128)}, u32[]{:S(2)}) copy-start(f32[512,128]{1,0:T(8,128)} %get-tuple-element.86) | copy-start | bytes 786436
  (10 other events, 11.2 us)

commit v2 on v1

v2 whole, which is shorter than its diff:
```python
import math

import jax
import jax.numpy as jnp
from jax import lax
from jax.experimental import pallas as pl
from jax.experimental.pallas import tpu as pltpu
from jax.sharding import PartitionSpec as P

WIDTH = 256
HEADDIM = 32
FF = 1024
PLAN_STEP_COUNT = 8
TOKENS = 256
NEIGHBOURS = 7
ROUNDS = 4
EPS = 1e-05
CAP = 4.0
ROOT = math.sqrt(HEADDIM)
GELU = math.sqrt(2 / math.pi)

MESH = pl.DeviceIdType.MESH
GROUP_ROWS = 4096
HALF = 2048
SMALL_ROWS = 16


class Place:
    def __init__(self):
        self.gx = lax.axis_index("gx")
        self.gy = lax.axis_index("gy")
        self.z = lax.rem(self.gx, 8)
        self.y_lo = lax.div(self.gx, 8)
        self.core = lax.rem(self.gy, 2)
        self.y_hi = lax.rem(lax.div(self.gy, 2), 2)
        self.x = lax.div(self.gy, 4)
        self.y = self.y_hi * 2 + self.y_lo

    def other_core(self):
        return (self.gx, self.gy + 1 - 2 * self.core)

    def at_x(self, x):
        return (self.gx, x * 4 + self.y_hi * 2 + self.core)

    def at_y(self, y):
        return (lax.rem(y, 2) * 8 + self.z, self.x * 4 + lax.div(y, 2) * 2 + self.core)

    def at_z(self, z):
        return (self.y_lo * 8 + z, self.gy)

    def greeted(self):
        peers = [self.other_core()]
        for step in range(1, 4):
            peers.append(self.at_x(lax.rem(self.x + step, 4)))
            peers.append(self.at_y(lax.rem(self.y + step, 4)))
        for step in range(1, 8):
            peers.append(self.at_z(lax.rem(self.z + step, 8)))
        for step in (1, 15):
            peers.append(self.row_tile(step))
            peers.append(self.column_tile(step))
        return peers

    def row_tile(self, step):
        return (lax.rem(self.gx + step, 16), self.gy)

    def column_tile(self, step):
        return (self.gx, lax.rem(self.gy + step, 16))


def greet(peers):
    barrier = pltpu.get_barrier_semaphore()
    for peer in peers:
        pl.semaphore_signal(barrier, inc=1, device_id=peer, device_id_type=MESH)
    return barrier, len(peers)


def rows(start, count):
    return pl.ds(pl.multiple_of(start, 16), count)


class Sum:
    SCRATCH = (
        pltpu.VMEM((HALF, 128), jnp.bfloat16),
        pltpu.VMEM((HALF, 128), jnp.bfloat16),
        pltpu.VMEM((6, 256, 128), jnp.bfloat16),
        pltpu.VMEM((2, 256, 128), jnp.bfloat16),
        pltpu.VMEM((6, 64, 128), jnp.bfloat16),
        pltpu.VMEM((128, 128), jnp.bfloat16),
        pltpu.VMEM((7, 16, 128), jnp.bfloat16),
        pltpu.SemaphoreType.DMA((40,)),
        pltpu.SemaphoreType.DMA((40,)),
    )

    def __init__(self, place, group, source, result, scratch):
        self.place = place
        self.source = source
        self.base = group * GROUP_ROWS
        self.result = result
        (self.from_core, self.one, self.in_two, self.two, self.in_three, self.three, self.in_four,
         self.send, self.recv) = scratch

    def copy(self, slot, source, target, peer):
        copy = pltpu.make_async_remote_copy(
            src_ref=source,
            dst_ref=target,
            send_sem=self.send.at[slot],
            recv_sem=self.recv.at[slot],
            device_id=peer,
            device_id_type=MESH,
        )
        copy.start()
        return copy

    def core_out(self):
        other = rows((1 - self.place.core) * HALF, HALF)
        self.core_copy = self.copy(0, self.source.at[other], self.from_core, self.place.other_core())

    def core_in(self):
        p = self.place
        self.core_copy.wait()
        own = self.source[rows(p.core * HALF, HALF)]
        self.one[...] = (own.astype(jnp.float32) + self.from_core[...].astype(jnp.float32)).astype(jnp.bfloat16)
        self.copies = []
        for step in range(1, 4):
            x, y = lax.rem(p.x + step, 4), lax.rem(p.y + step, 4)
            self.copies.append(
                self.copy(step, self.one.at[rows(x * 256, 256)], self.in_two.at[step - 1], p.at_x(x)))
            self.copies.append(
                self.copy(3 + step, self.one.at[rows(1024 + y * 256, 256)], self.in_two.at[2 + step], p.at_y(y)))

    def two_in(self):
        p = self.place
        for copy in self.copies:
            copy.wait()
        for part, own in ((0, p.x * 256), (1, 1024 + p.y * 256)):
            total = self.one[rows(own, 256)].astype(jnp.float32)
            for step in range(3):
                total = total + self.in_two[part * 3 + step].astype(jnp.float32)
            self.two[part] = total.astype(jnp.bfloat16)
        self.copies = []
        for step in range(1, 4):
            x, y = lax.rem(p.x + step, 4), lax.rem(p.y + step, 4)
            self.copies.append(
                self.copy(6 + step, self.two.at[0, rows(y * 64, 64)], self.in_three.at[step - 1], p.at_y(y)))
            self.copies.append(
                self.copy(9 + step, self.two.at[1, rows(x * 64, 64)], self.in_three.at[2 + step], p.at_x(x)))

    def three_in(self):
        p = self.place
        for copy in self.copies:
            copy.wait()
        for part, own in ((0, p.y * 64), (1, p.x * 64)):
            total = self.two[part, rows(own, 64)].astype(jnp.float32)
            for step in range(3):
                total = total + self.in_three[part * 3 + step].astype(jnp.float32)
            self.three[part * 64 : part * 64 + 64] = total.astype(jnp.bfloat16)
        self.copies = []
        for step in range(1, 8):
            z = lax.rem(p.z + step, 8)
            self.copies.append(
                self.copy(12 + step, self.three.at[rows(z * 16, 16)], self.in_four.at[step - 1], p.at_z(z)))

    def four_in(self):
        p = self.place
        for copy in self.copies:
            copy.wait()
        total = self.three[rows(p.z * 16, 16)].astype(jnp.float32)
        for step in range(7):
            total = total + self.in_four[step].astype(jnp.float32)
        half = self.base + p.core * HALF
        self.first = half + p.x * 256 + p.y * 64
        self.second = half + 1024 + p.y * 256 + p.x * 64
        upper = lax.div(p.z, 4)
        own = (1 - upper) * self.first + upper * self.second + lax.rem(p.z, 4) * 16
        self.result[rows(own, 16)] = total.astype(jnp.bfloat16)
        self.copies = []
        for step in range(1, 8):
            z = lax.rem(p.z + step, 8)
            tile = self.result.at[rows(own, 16)]
            self.copies.append(self.copy(19 + step, tile, tile, p.at_z(z)))

    def z_gathered(self):
        p = self.place
        for copy in self.copies:
            copy.wait()
        first, second = self.result.at[rows(self.first, 64)], self.result.at[rows(self.second, 64)]
        self.copies = []
        for step in range(1, 4):
            x, y = lax.rem(p.x + step, 4), lax.rem(p.y + step, 4)
            self.copies.append(self.copy(26 + step, first, first, p.at_y(y)))
            self.copies.append(self.copy(29 + step, second, second, p.at_x(x)))

    def one_gathered(self):
        p = self.place
        for copy in self.copies:
            copy.wait()
        half = self.base + p.core * HALF
        first = self.result.at[rows(half + p.x * 256, 256)]
        second = self.result.at[rows(half + 1024 + p.y * 256, 256)]
        self.copies = []
        for step in range(1, 4):
            x, y = lax.rem(p.x + step, 4), lax.rem(p.y + step, 4)
            self.copies.append(self.copy(32 + step, first, first, p.at_x(x)))
            self.copies.append(self.copy(35 + step, second, second, p.at_y(y)))

    def both_gathered(self):
        p = self.place
        for copy in self.copies:
            copy.wait()
        own = self.result.at[rows(self.base + p.core * HALF, HALF)]
        self.core_copy = self.copy(39, own, own, p.other_core())

    def finish(self):
        self.core_copy.wait()


class SmallSum:
    SCRATCH = (
        pltpu.VMEM((2, SMALL_ROWS, 256), jnp.float32),
        pltpu.VMEM((4, SMALL_ROWS, 256), jnp.float32),
        pltpu.VMEM((4, SMALL_ROWS, 256), jnp.float32),
        pltpu.VMEM((8, SMALL_ROWS, 256), jnp.float32),
        pltpu.SemaphoreType.DMA((14,)),
        pltpu.SemaphoreType.DMA((14,)),
    )

    def __init__(self, place, scratch):
        self.place = place
        self.slots = scratch[:4]
        self.send, self.recv = scratch[4:]
        self.stage = -1

    def out(self, value):
        p = self.place
        self.stage += 1
        slots = self.slots[self.stage]
        mine = (p.core, p.x, p.y, p.z)[self.stage]
        at = (lambda _: p.other_core(), p.at_x, p.at_y, p.at_z)[self.stage]
        first = (0, 1, 4, 7)[self.stage]
        count = slots.shape[0]
        slots[mine] = value
        self.copies = []
        for step in range(1, count):
            copy = pltpu.make_async_remote_copy(
                src_ref=slots.at[mine],
                dst_ref=slots.at[mine],
                send_sem=self.send.at[first + step - 1],
                recv_sem=self.recv.at[first + step - 1],
                device_id=at(lax.rem(mine + step, count)),
                device_id_type=MESH,
            )
            copy.start()
            self.copies.append(copy)

    def total(self):
        for copy in self.copies:
            copy.wait()
        slots = self.slots[self.stage]
        total = slots[0]
        for index in range(1, slots.shape[0]):
            total = total + slots[index]
        return total


def dot(left, right):
    return lax.dot_general(left, right, (((1,), (0,)), ((), ())), preferred_element_type=jnp.float32)


def dot_back(grad, weight):
    return lax.dot_general(grad, weight, (((1,), (1,)), ((), ())), preferred_element_type=jnp.float32)


def dot_weight(inputs, grad):
    return lax.dot_general(inputs, grad, (((0,), (0,)), ((), ())), preferred_element_type=jnp.float32)


def low(value):
    return value.astype(jnp.bfloat16)


def wide(value):
    return value.astype(jnp.float32)


def halves(value):
    upper = low(value)
    return upper, low(value - wide(upper))


def ones(mask):
    return low(jnp.where(mask, 1.0, 0.0))


def iota(shape, axis):
    return lax.broadcasted_iota(jnp.int32, shape, axis)


def norm(stream, gain):
    inverse = lax.rsqrt(jnp.mean(stream * stream, axis=-1, keepdims=True) + EPS)
    unit = stream * inverse
    return unit, inverse, low(unit * gain)


def norm_back(grad, unit, inverse, gain):
    scaled = grad * gain
    along = jnp.mean(scaled * unit, axis=-1, keepdims=True)
    return inverse * (scaled - unit * along), jnp.sum(grad * unit, axis=0, keepdims=True)


def over_neighbours(value):
    value = value + pltpu.roll(value, 64, 1)
    value = value + pltpu.roll(value, 32, 1)
    return value + pltpu.roll(value, 16, 1)


class Attention:
    def __init__(self, gather_ref, spread_ref, count, key, value, allowed):
        self.gather_ref = gather_ref
        self.spread_ref = spread_ref
        self.count = count
        self.key = key
        self.value = value
        self.allowed = allowed

    def gather(self, products):
        total = jnp.zeros((TOKENS, 128), jnp.float32)
        for index in range(self.count):
            matrix = self.gather_ref[index * WIDTH : (index + 1) * WIDTH]
            upper, lower = halves(products(index))
            total = total + dot(upper, matrix) + dot(lower, matrix)
        return total

    def spread(self, small, index):
        both = jnp.concatenate(halves(small), axis=1)
        return dot(both, self.spread_ref[:, index * WIDTH : (index + 1) * WIDTH])

    def forward(self, query):
        score = self.gather(lambda index: query * self.key(index))
        self.capped = jnp.tanh(score * (1.0 / (ROOT * CAP)))
        weight = jnp.where(self.allowed, jnp.exp(CAP * self.capped), 0.0)
        self.share = weight / over_neighbours(weight)
        mixed = jnp.zeros((TOKENS, WIDTH), jnp.float32)
        for index in range(self.count):
            mixed = mixed + self.spread(self.share, index) * self.value(index)
        return mixed

    def backward(self, query, grad, put):
        grad_share = self.gather(lambda index: grad * self.value(index))
        along = over_neighbours(self.share * grad_share)
        grad_score = self.share * (grad_share - along) * (1.0 - self.capped * self.capped) * (1.0 / ROOT)
        grad_query = jnp.zeros((TOKENS, WIDTH), jnp.float32)
        for index in range(self.count):
            spread = self.spread(grad_score, index)
            grad_query = grad_query + spread * self.key(index)
            put(index, spread * query, self.spread(self.share, index) * grad)
        return grad_query


def turn(value, by):
    return pltpu.roll(value.reshape(TOKENS // 8, 8, -1), by, 1).reshape(TOKENS, -1)


def window_kernel(
    tokens_ref,
    syndrome_ref,
    step_ref,
    offsets_ref,
    flip_ref,
    embedding_ref,
    gain_tanner_ref,
    w_query_ref,
    w_key_value_ref,
    w_merge_ref,
    gain_time_ref,
    w_temporal_ref,
    w_temporal_out_ref,
    gain_ffn_ref,
    w_up_ref,
    w_down_ref,
    cotangent_ref,
    result_ref,
    small_result_ref,
    token_grad_ref,
    early_ref,
    late_ref,
    gather_ref,
    spread_ref,
    hidden_ref,
    back_out_ref,
    back_in_ref,
    ahead_ref,
    near_ref,
    padded_ref,
    grad_key_value_ref,
    activated_ref,
    before_ref,
    packed_ref,
    grad_packed_ref,
    halo_send,
    halo_recv,
    *scratch,
):
    place = Place()
    barrier, greeted = greet(place.greeted())
    per = len(Sum.SCRATCH)
    early = Sum(place, 0, early_ref, result_ref, scratch[:per])
    late = Sum(place, 1, late_ref, result_ref, scratch[per : 2 * per])
    small = SmallSum(place, scratch[2 * per :])

    def send(slot, source, target, peer):
        copy = pltpu.make_async_remote_copy(
            src_ref=source,
            dst_ref=target,
            send_sem=halo_send.at[slot],
            recv_sem=halo_recv.at[slot],
            device_id=peer,
            device_id_type=MESH,
        )
        copy.start()
        return copy

    code = low(wide(step_ref[...] + 16 * syndrome_ref[...]))
    site_row = ones(lax.div(iota((TOKENS, 32), 0), 8) == iota((TOKENS, 32), 1))
    site_column = lax.rem(iota((TOKENS, 8), 0), 8) == iota((TOKENS, 8), 1)
    code = jnp.sum(jnp.where(site_column, dot(site_row, code), 0.0), axis=1, keepdims=True)
    lane = iota((TOKENS, 16), 1)
    lane_value = wide(lane)
    flipped = jnp.where(code > 15.5, 1.0, 0.0)
    on_step = jnp.where(code - 16.0 * flipped == lane_value, 1.0, 0.0)
    features = low(jnp.where(lane < 8, on_step, jnp.where(lane == 8, flipped, 0.0)))
    table = jnp.concatenate(
        [embedding_ref[...], jnp.broadcast_to(flip_ref[...], (8, WIDTH))], axis=0)
    upper = low(table)
    middle, lower = halves(table - wide(upper))
    embedded = wide(tokens_ref[...]) + (dot(features, upper) + (dot(features, middle) + dot(features, lower)))
    unit_one, inverse_one, hidden_one = norm(embedded, gain_tanner_ref[...])
    hidden_ref[:TOKENS] = hidden_one
    pl.semaphore_wait(barrier, greeted)
    own_hidden = hidden_ref.at[pl.ds(0, TOKENS)]
    ahead_rows = send(0, own_hidden, hidden_ref.at[pl.ds(TOKENS, TOKENS)], place.row_tile(15))
    ahead_columns = send(1, own_hidden, hidden_ref.at[pl.ds(2 * TOKENS, TOKENS)], place.column_tile(15))

    shape = (NEIGHBOURS * WIDTH, 128)
    feature = iota(shape, 0)
    gather_ref[...] = ones(
        lax.div(feature, WIDTH) * 16 + lax.div(lax.rem(feature, WIDTH), HEADDIM) == iota(shape, 1))
    shape = (256, NEIGHBOURS * WIDTH)
    feature = iota(shape, 1)
    spread_ref[...] = ones(
        lax.div(feature, WIDTH) * 16 + lax.div(lax.rem(feature, WIDTH), HEADDIM) == lax.rem(iota(shape, 0), 128))

    query = wide(low(dot(hidden_one, w_query_ref[...])))
    own = wide(low(dot(hidden_one, w_key_value_ref[...])))
    near_ref[0] = own
    ahead_ref[:, 0:8] = own.reshape(ROUNDS, 8, 8, 2 * WIDTH)
    ahead_rows.wait()
    rows_ahead = wide(low(dot(hidden_ref[TOKENS : 2 * TOKENS], w_key_value_ref[...])))
    near_ref[1] = rows_ahead
    ahead_ref[:, 8:16] = rows_ahead.reshape(ROUNDS, 8, 8, 2 * WIDTH)
    for index in (5, 6):
        near_ref[index] = ahead_ref[:, pl.ds(offsets_ref[index - 1, 0], 8)].reshape(TOKENS, 2 * WIDTH)
    ahead_columns.wait()
    columns_ahead = wide(low(dot(hidden_ref[2 * TOKENS :], w_key_value_ref[...])))
    near_ref[4] = columns_ahead
    column = lax.rem(iota((TOKENS, 1), 0), 8)
    for index in (2, 3):
        by = offsets_ref[index - 1, 1]
        near_ref[index] = jnp.where(column < 8 - by, turn(own, 8 - by), turn(columns_ahead, 8 - by))
    lanes = iota((TOKENS, 128), 1)
    tanner = Attention(
        gather_ref,
        spread_ref,
        NEIGHBOURS,
        lambda index: near_ref[index, :, :WIDTH],
        lambda index: near_ref[index, :, WIDTH:],
        lanes < NEIGHBOURS * 16,
    )
    mixed_one = low(tanner.forward(query))
    after_tanner = embedded + dot(mixed_one, w_merge_ref[...])

    unit_two, inverse_two, hidden_two = norm(after_tanner, gain_time_ref[...])
    packed_ref[...] = wide(low(dot(hidden_two, w_temporal_ref[...])))
    time_query = packed_ref[:, :WIDTH]

    def of_round(index, column):
        value = packed_ref[index * 64 : index * 64 + 64, column : column + WIDTH]
        return jnp.concatenate([value] * ROUNDS, axis=0)

    temporal = Attention(
        gather_ref,
        spread_ref,
        ROUNDS,
        lambda index: of_round(index, WIDTH),
        lambda index: of_round(index, 2 * WIDTH),
        lax.div(lanes, 16) <= lax.div(iota((TOKENS, 128), 0), 64),
    )
    mixed_two = low(temporal.forward(time_query))
    after_time = after_tanner + dot(mixed_two, w_temporal_out_ref[...])

    def put(target, slab, value):
        for half in range(value.shape[1] // 128):
            target[(slab + half) * 256 : (slab + half + 1) * 256] = low(value[:, half * 128 : half * 128 + 128])

    unit_three, inverse_three, hidden_three = norm(after_time, gain_ffn_ref[...])
    cotangent = cotangent_ref[...]
    for block in range(FF // WIDTH):
        part = slice(block * WIDTH, (block + 1) * WIDTH)
        before = dot(hidden_three, w_up_ref[:, part])
        square = before * before
        bend = jnp.tanh(GELU * before * (1.0 + 0.044715 * square))
        activated_ref[:, part] = low(0.5 * before * (1.0 + bend))
        slope = 0.5 * (1.0 + bend) + 0.5 * before * (1.0 - bend * bend) * (GELU * (1.0 + 3 * 0.044715 * square))
        before_ref[:, part] = low(dot_back(cotangent, w_down_ref[part]) * slope)
    for block in range(FF // WIDTH):
        part = slice(block * WIDTH, (block + 1) * WIDTH)
        put(early_ref, 2 * block, dot_weight(activated_ref[:, part], cotangent))
    put(early_ref, 8, dot_weight(hidden_three, before_ref[...]))
    early.core_out()
    grad_three = dot_back(before_ref[...], w_up_ref[...])
    grad_norm, grad_gain_ffn = norm_back(grad_three, unit_three, inverse_three, gain_ffn_ref[...])
    grad_after_time = wide(cotangent) + grad_norm

    grad_low = low(grad_after_time)
    put(late_ref, 14, dot_weight(mixed_two, grad_low))
    grad_mixed = dot_back(grad_low, w_temporal_out_ref[...])
    early.core_in()

    def over_rounds(value):
        return (value[:64] + value[64:128]) + (value[128:192] + value[192:])

    def put_time(index, grad_key, grad_value):
        grad_packed_ref[index * 64 : index * 64 + 64, WIDTH : 2 * WIDTH] = low(over_rounds(grad_key))
        grad_packed_ref[index * 64 : index * 64 + 64, 2 * WIDTH :] = low(over_rounds(grad_value))

    grad_packed_ref[:, :WIDTH] = low(temporal.backward(time_query, grad_mixed, put_time))
    put(late_ref, 8, dot_weight(hidden_two, grad_packed_ref[...]))
    grad_two = dot_back(grad_packed_ref[...], w_temporal_ref[...])
    grad_norm, grad_gain_time = norm_back(grad_two, unit_two, inverse_two, gain_time_ref[...])
    grad_after_tanner = grad_after_time + grad_norm
    early.two_in()

    grad_low = low(grad_after_tanner)
    put(late_ref, 6, dot_weight(mixed_one, grad_low))
    grad_mixed = dot_back(grad_low, w_merge_ref[...])
    for index in range(2):
        padded_ref[index, :, 0:8] = jnp.zeros((ROUNDS, 8, 8, 2 * WIDTH), jnp.float32)
        padded_ref[index, :, 16:24] = jnp.zeros((ROUNDS, 8, 8, 2 * WIDTH), jnp.float32)

    def put_tanner(index, grad_key, grad_value):
        grad = jnp.concatenate([grad_key, grad_value], axis=1)
        if index == 0:
            grad_key_value_ref[0] = grad
        elif index == 1:
            grad_key_value_ref[1] = grad
        elif index == 4:
            grad_key_value_ref[2] = grad
        elif index in (2, 3):
            by = offsets_ref[index - 1, 1]
            turned = turn(grad, by)
            near_ref[index] = jnp.where(column >= by, turned, 0.0)
            near_ref[index + 2] = jnp.where(column >= by, 0.0, turned)
        else:
            padded_ref[index - 5, :, 8:16] = grad.reshape(ROUNDS, 8, 8, 2 * WIDTH)

    kept = {}

    def hold(index, grad_key, grad_value):
        kept[index] = (grad_key, grad_value)

    grad_query = tanner.backward(query, grad_mixed, hold)
    for index in (0, 1, 4, 5, 6, 2, 3):
        put_tanner(index, *kept[index])
    own_grad = grad_key_value_ref[0] + near_ref[2] + near_ref[3]
    rows_grad = grad_key_value_ref[1]
    for index in (5, 6):
        by = offsets_ref[index - 1, 0]
        own_grad = own_grad + padded_ref[index - 5, :, pl.ds(8 - by, 8)].reshape(TOKENS, 2 * WIDTH)
        rows_grad = rows_grad + padded_ref[index - 5, :, pl.ds(16 - by, 8)].reshape(TOKENS, 2 * WIDTH)
    columns_grad = grad_key_value_ref[2] + near_ref[4] + near_ref[5]
    rows_low, columns_low, own_low = low(rows_grad), low(columns_grad), low(own_grad)
    back_out_ref[0] = low(dot_back(rows_low, w_key_value_ref[...]))
    back_rows = send(2, back_out_ref.at[0], back_in_ref.at[0], place.row_tile(1))
    back_out_ref[1] = low(dot_back(columns_low, w_key_value_ref[...]))
    back_columns = send(3, back_out_ref.at[1], back_in_ref.at[1], place.column_tile(1))
    early.three_in()
    query_low = low(grad_query)
    put(late_ref, 0, dot_weight(hidden_one, query_low))
    put(
        late_ref,
        2,
        dot_weight(hidden_one, own_low)
        + dot_weight(hidden_ref[TOKENS : 2 * TOKENS], rows_low)
        + dot_weight(hidden_ref[2 * TOKENS :], columns_low),
    )
    late.core_out()
    early.four_in()
    grad_one = dot_back(query_low, w_query_ref[...]) + dot_back(own_low, w_key_value_ref[...])
    late.core_in()
    back_rows.wait()
    back_columns.wait()
    grad_one = grad_one + (wide(back_in_ref[0]) + wide(back_in_ref[1]))
    grad_norm, grad_gain_tanner = norm_back(grad_one, unit_one, inverse_one, gain_tanner_ref[...])
    grad_embedded = grad_after_tanner + grad_norm
    token_grad_ref[...] = low(grad_embedded)
    upper, lower = halves(grad_embedded)
    from_table = dot_weight(features, upper) + dot_weight(features, lower)
    row = iota((SMALL_ROWS, WIDTH), 0)
    shares = jnp.where(row == 9, grad_gain_tanner, from_table)
    shares = jnp.where(row == 10, grad_gain_time, shares)
    shares = jnp.where(row == 11, grad_gain_ffn, shares)
    small.out(shares)
    early.z_gathered()
    late.two_in()
    small.out(small.total())
    early.one_gathered()
    late.three_in()
    small.out(small.total())
    early.both_gathered()
    late.four_in()
    small.out(small.total())
    late.z_gathered()
    small_result_ref[...] = small.total()
    late.one_gathered()
    late.both_gathered()
    early.finish()
    late.finish()


def window(*operands):
    vmem = pl.BlockSpec(memory_space=pltpu.VMEM)
    specs = [vmem] * len(operands)
    specs[3] = pl.BlockSpec(memory_space=pltpu.SMEM)
    bf16, f32 = jnp.bfloat16, jnp.float32
    return pl.pallas_call(
        window_kernel,
        name="window",
        out_shape=(
            jax.ShapeDtypeStruct((2 * GROUP_ROWS, 128), bf16),
            jax.ShapeDtypeStruct((SMALL_ROWS, WIDTH), f32),
            jax.ShapeDtypeStruct((TOKENS, WIDTH), bf16),
        ),
        in_specs=specs,
        out_specs=(vmem, vmem, vmem),
        scratch_shapes=[
            pltpu.VMEM((GROUP_ROWS, 128), bf16),
            pltpu.VMEM((GROUP_ROWS, 128), bf16),
            pltpu.VMEM((NEIGHBOURS * WIDTH, 128), bf16),
            pltpu.VMEM((256, NEIGHBOURS * WIDTH), bf16),
            pltpu.VMEM((3 * TOKENS, WIDTH), bf16),
            pltpu.VMEM((2, TOKENS, WIDTH), bf16),
            pltpu.VMEM((2, TOKENS, WIDTH), bf16),
            pltpu.VMEM((ROUNDS, 16, 8, 2 * WIDTH), f32),
            pltpu.VMEM((NEIGHBOURS, TOKENS, 2 * WIDTH), f32),
            pltpu.VMEM((2, ROUNDS, 24, 8, 2 * WIDTH), f32),
            pltpu.VMEM((3, TOKENS, 2 * WIDTH), f32),
            pltpu.VMEM((TOKENS, FF), bf16),
            pltpu.VMEM((TOKENS, FF), bf16),
            pltpu.VMEM((TOKENS, 3 * WIDTH), f32),
            pltpu.VMEM((TOKENS, 3 * WIDTH), bf16),
            pltpu.SemaphoreType.DMA((4,)),
            pltpu.SemaphoreType.DMA((4,)),
            *Sum.SCRATCH,
            *Sum.SCRATCH,
            *SmallSum.SCRATCH,
        ],
        compiler_params=pltpu.CompilerParams(
            collective_id=0, has_side_effects=True, vmem_limit_bytes=56 * 2**20),
    )(*operands)


def finish_kernel(scale, slabs_ref, small_ref, token_grad_in_ref, *outs):
    (token_grad_ref, flip_ref, plan_ref, gain_tanner_ref, query_ref, key_value_ref, merge_ref,
     gain_time_ref, temporal_ref, temporal_out_ref, gain_ffn_ref, up_ref, down_ref) = outs
    token_grad_ref[...] = token_grad_in_ref[...]
    small = small_ref[...] * scale
    plan_ref[...] = small[:8]
    flip_ref[...] = small[8:9]
    gain_tanner_ref[...] = small[9:10]
    gain_time_ref[...] = small[10:11]
    gain_ffn_ref[...] = small[11:12]

    def take(target, slab):
        for block in range(target.shape[0] // 256):
            for half in range(target.shape[1] // 128):
                target[block * 256 : block * 256 + 256, half * 128 : half * 128 + 128] = (
                    wide(slabs_ref[slab * 256 : slab * 256 + 256]) * scale)
                slab += 1

    take(down_ref, 0)
    take(up_ref, 8)
    take(query_ref, 16)
    take(key_value_ref, 18)
    take(merge_ref, 22)
    take(temporal_ref, 24)
    take(temporal_out_ref, 30)


def finish(scale, slabs, small, token_grad):
    vmem = pl.BlockSpec(memory_space=pltpu.VMEM)
    f32 = jnp.float32
    return pl.pallas_call(
        lambda *refs: finish_kernel(scale, *refs),
        name="finish",
        out_shape=(
            jax.ShapeDtypeStruct((TOKENS, WIDTH), jnp.bfloat16),
            jax.ShapeDtypeStruct((1, WIDTH), f32),
            jax.ShapeDtypeStruct((PLAN_STEP_COUNT, WIDTH), f32),
            jax.ShapeDtypeStruct((1, WIDTH), f32),
            jax.ShapeDtypeStruct((WIDTH, WIDTH), f32),
            jax.ShapeDtypeStruct((WIDTH, 2 * WIDTH), f32),
            jax.ShapeDtypeStruct((WIDTH, WIDTH), f32),
            jax.ShapeDtypeStruct((1, WIDTH), f32),
            jax.ShapeDtypeStruct((WIDTH, 3 * WIDTH), f32),
            jax.ShapeDtypeStruct((WIDTH, WIDTH), f32),
            jax.ShapeDtypeStruct((1, WIDTH), f32),
            jax.ShapeDtypeStruct((WIDTH, FF), f32),
            jax.ShapeDtypeStruct((FF, WIDTH), f32),
        ),
        in_specs=[vmem] * 3,
        out_specs=(vmem,) * 13,
        compiler_params=pltpu.CompilerParams(vmem_limit_bytes=32 * 2**20),
    )(slabs, small, token_grad)


def on_device(
    tokens,
    syndrome,
    check_plan_step,
    offsets,
    flip_vector,
    plan_step_embedding,
    gain_tanner,
    w_query,
    w_key_value,
    w_merge,
    gain_time,
    w_temporal,
    w_temporal_out,
    gain_ffn,
    w_ffn_up,
    w_ffn_down,
    cotangent,
):
    tile = tokens.shape
    devices = lax.axis_size("gx") * lax.axis_size("gy")
    scale = 1.0 / math.sqrt(tile[0] * tile[1] * tile[2] * devices)
    slabs, small, token_grad = window(
        tokens.reshape(TOKENS, WIDTH),
        syndrome.reshape(TOKENS // 8, 8),
        check_plan_step.reshape(TOKENS // 8, 8),
        offsets,
        flip_vector.reshape(1, WIDTH),
        plan_step_embedding,
        gain_tanner.reshape(1, WIDTH),
        w_query,
        w_key_value,
        w_merge,
        gain_time.reshape(1, WIDTH),
        w_temporal,
        w_temporal_out,
        gain_ffn.reshape(1, WIDTH),
        w_ffn_up,
        w_ffn_down,
        cotangent.reshape(TOKENS, WIDTH),
    )
    outs = list(finish(scale, slabs, small, token_grad))
    outs[0] = outs[0].reshape(tile)
    for index in (1, 3, 7, 10):
        outs[index] = outs[index].reshape(WIDTH)
    return tuple(outs)


def solution(mesh):
    return jax.shard_map(
        on_device,
        mesh=mesh,
        in_specs=(
            P(None, "gx", "gy", None),
            P(None, "gx", "gy"),
            P(None, "gx", "gy"),
            P(),
            P(),
            P(),
            P(),
            P(),
            P(),
            P(),
            P(),
            P(),
            P(),
            P(),
            P(),
            P(),
            P(None, "gx", "gy", None),
        ),
        out_specs=(
            P(None, "gx", "gy", None),
            P(),
            P(),
            P(),
            P(),
            P(),
            P(),
            P(),
            P(),
            P(),
            P(),
            P(),
            P(),
        ),
        check_vma=False,
    )
```

time: 142 us -> 79.7 us (0.56)
  matrix products: 34.3 us -> 0 us
  Pallas kernels: 44 us -> 74.3 us
  local copies, waits for them, and re-layouts: 25.4 us -> 4.56 us
  other arithmetic: 13 us -> 0 us
  between operations: 13.6 us -> 0.66 us
  starting transfers between devices: 11 us -> 0 us
    dot_general x56 -> x0, matrix products: 34.3 us -> none  [the longest x34 15.5 us: head_total(): lax.dot_general(product, block, (((product.ndim - 1,), (0,)), ((), ())),...]
    pallas_call x1 -> x2, Pallas kernels: 44 us -> 74.3 us  [the longest x1 72 us: window(): pl.pallas_call(window_kernel, name='window', out_shape=(jax.ShapeDtypeStr...]
    ppermute x4 -> x0, starting transfers between devices: 11 us -> none  [shifted(): return lax.ppermute(x, axis, [(i, (i + by) % count) for i in range(count)])]
    dot_general x8 -> x0, local copies, waits for them, and re-layouts: 5.81 us -> none  [back_matmul(): lax.dot_general(flat_inputs, flat_grad, (((0,), (0,)), ((), ())), preferr...]
    convert_element_type x11 -> x0, other arithmetic: 5.38 us -> none  [the longest x4 2.84 us: back_matmul(): grad_low = grad_result.astype(jnp.bfloat16)]
    unnamed x119 -> x7, local copies, waits for them, and re-layouts: 9.73 us -> 4.56 us
    dynamic_update_slice x3 -> x0, other arithmetic: 3.34 us -> none  [the longest x2 2.33 us: tanner_local(): lax.dynamic_slice_in_dim(extended_cols, offsets[index, 1], key_value.shap...]
    mul x7 -> x0, local copies, waits for them, and re-layouts: 2.63 us -> none  [from_slabs(): grads.append(piece.reshape(depth, width).astype(jnp.float32) * scale)]
  transfers between devices with their start and end apart: 4 -> 0, of which waited for: 0 -> 0; matrix products, arithmetic and copies ran while one was open for 11% -> 0% of each run, Pallas kernels for 0% -> 0%
where the time goes in v2:
time: 79.7 us; the launch traced here: 79.5 us
  Pallas kernels  74.3 us (93%)
  local copies, waits for them, and re-layouts  4.56 us (6%)
    pallas_call x1, Pallas kernels, window(): pl.pallas_call(window_kernel, name='window', out_shape=(jax.ShapeDtypeStr...  72 us
    unnamed x7, local copies, waits for them, and re-layouts  4.56 us
    pallas_call x1, Pallas kernels, finish(): pl.pallas_call(lambda *refs: finish_kernel(scale, *refs), name='finish',...  2.25 us

profile of v2, /device:TPU:1, one launch (start us, length us, event | category | flops | bytes accessed | tf_op | source)
XLA Modules:
  0.0 79.5 jit_solution(6918019714949687510)
XLA Ops:
  0.6 1.4 %copy.30.offsets_ref = s32[6,2]{1,0:T(8,128)} copy(s32[6,2]{0,1:T(2,128)} %param.20) | data formatting | bytes 96 | tf_op args[3]
  2.0 72.0 %window.1 = (bf16[8192,128]{1,0:T(8,128)(2,1)}, f32[16,256]{1,0:T(8,128)}, bf16[256,256]{1,0:T(8,128)(2,1)}) custom-call(bf16[256,256]{1,0:T(8,128)(2,1)} %bitcast.13, s32[32,8]{1,0:T(8,128)} %bitcast.15, s32[32,8]{1,0:T(8,128)} %bitcast.16, s32[6,2]{1,0:T(8,128)} %copy.30.offsets_ref, f32[1,256]{1,0:T(1,128)} %bitcast.17, f32[8,256]{1,0:T(8,128)} %embedding_ref.1, ...), custom_call_target="tpu_custom_call" | custom-call | tf_op jit(solution)/shard_map/window/pallas_call | solution.py:634
  74.0 0.0 copy-start
  74.0 1.6 %copy-done = bf16[8192,128]{1,0:T(8,128)(2,1)S(1)} copy-done((bf16[8192,128]{1,0:T(8,128)(2,1)S(1)}, bf16[8192,128]{1,0:T(8,128)(2,1)}, u32[]{:S(2)}) %copy-start) | copy-done | bytes 2097176
  75.6 0.0 copy-start.1
  75.6 0.9 %copy-done.1 = bf16[256,256]{1,0:T(8,128)(2,1)S(1)} copy-done((bf16[256,256]{1,0:T(8,128)(2,1)S(1)}, bf16[256,256]{1,0:T(8,128)(2,1)}, u32[]{:S(2)}) %copy-start.1) | copy-done | bytes 131096
  76.5 0.0 copy-start.2
  76.5 0.7 copy-done.2
  77.2 2.3 %finish.1 = (bf16[256,256]{1,0:T(8,128)(2,1)}, f32[1,256]{1,0:T(1,128)}, f32[8,256]{1,0:T(8,128)}, f32[1,256]{1,0:T(1,128)}, f32[256,256]{1,0:T(8,128)}, /*index...) custom-call(bf16[8192,128]{1,0:T(8,128)(2,1)S(1)} %copy-done, ...), custom_call_target="tpu_custom_call" | custom-call | tf_op jit(solution)/shard_map/finish/pallas_call | solution.py:701
Async XLA Ops:
  74.0 1.6 %copy-start = (bf16[8192,128]{1,0:T(8,128)(2,1)S(1)}, bf16[8192,128]{1,0:T(8,128)(2,1)}, u32[]{:S(2)}) copy-start(bf16[8192,128]{1,0:T(8,128)(2,1)} %get-tuple-element.29.refs_0_) | copy-start | bytes 6291460
  75.6 0.9 %copy-start.1 = (bf16[256,256]{1,0:T(8,128)(2,1)S(1)}, bf16[256,256]{1,0:T(8,128)(2,1)}, u32[]{:S(2)}) copy-start(bf16[256,256]{1,0:T(8,128)(2,1)} %get-tuple-element.31.refs_2_) | copy-start | bytes 393220
  76.5 0.7 copy-start.2
